TPU v7x, 32 devices: a whole 2x2x4 slice. The times are simulated.
32 devices in a mesh: dp: 8 (over y, x, core), tensor: 4 (over z).
Axes of the slice: x: 2, y: 2, z: 4, core: 2. Of those that a mesh axis runs over, the one named last changes fastest.
Arguments:
- activations: bfloat16 [16, 1024, 1024], P('dp', 'tensor'), may hold values from -6 to 6
- cotangent: bfloat16 [16, 1024, 1024], P('dp', 'tensor'), may hold values from -6 to 6
- attn_gain: float32 [1024], replicated, may hold values from 0.5 to 1.5
- attn_shift: float32 [1024], replicated, may hold values from -2 to 2
- qkv_weight: bfloat16 [1024, 3072], P('dp', 'tensor'), may hold values from -0.1875 to 0.1875
- qkv_bias: float32 [3072], P('tensor'), may hold values from -3 to 3
- out_weight: bfloat16 [1024, 1024], P('dp', 'tensor'), may hold values from -3.5 to 3.5
- out_bias: float32 [1024], replicated, may hold values from -2 to 2
- mlp_gain: float32 [1024], replicated, may hold values from 0.5 to 1.5
- mlp_shift: float32 [1024], replicated, may hold values from -2 to 2
- fc1_weight: bfloat16 [1024, 4096], P('dp', 'tensor'), may hold values from -0.1875 to 0.1875
- fc1_bias: float32 [4096], P('tensor'), may hold values from -3 to 3
- fc2_weight: bfloat16 [1024, 4096], P('dp', 'tensor'), may hold values from -0.09375 to 0.09375
- fc2_bias: float32 [1024], replicated, may hold values from -2 to 2
Outputs:
- output: bfloat16 [16, 1024, 1024], P('dp', 'tensor')
- input_grad: float32 [16, 1024, 1024], P('dp', 'tensor')
- grad_attn_gain: float32 [1024], replicated
- grad_attn_shift: float32 [1024], replicated
- grad_qkv_weight: float32 [1024, 3072], P('dp', 'tensor')
- grad_qkv_bias: float32 [3072], P('tensor')
- grad_out_weight: float32 [1024, 1024], P('dp', 'tensor')
- grad_out_bias: float32 [1024], replicated
- grad_mlp_gain: float32 [1024], replicated
- grad_mlp_shift: float32 [1024], replicated
- grad_fc1_weight: float32 [1024, 4096], P('dp', 'tensor')
- grad_fc1_bias: float32 [4096], P('tensor')
- grad_fc2_weight: float32 [1024, 4096], P('dp', 'tensor')
- grad_fc2_bias: float32 [1024], replicated
All inputs are finite; a program needn't handle non-finite values.
Results may differ from a plain program's by a relative error of at most 0.02.
Values may be sent and summed in bfloat16 or wider, within the bound.
No kernel may reach another device: no remote copies, remote signals or barrier semaphores. Data moves between devices by JAX's collectives and lax.ppermute only.
A program may use at most 192 MiB of HBM per device.

v0:
```python
import math
import jax
import jax.numpy as jnp
from jax import lax
from jax.sharding import PartitionSpec as P

HD = 64
GRID = 16


def norm_rows(values, gain_vec, shift_vec):
    row_mean = jnp.mean(values, axis=-1, keepdims=True)
    centred = values - row_mean
    variance = jnp.mean(centred * centred, axis=-1, keepdims=True)
    return centred * lax.rsqrt(variance + 1e-06) * gain_vec + shift_vec


def rotary_tables(length):
    section = 2 * (HD // 3 // 2)
    half = section // 2
    position = jnp.arange(length)
    frame = (position // (GRID * GRID)).astype(jnp.float32)
    row_pos = (position // GRID % GRID).astype(jnp.float32)
    col_pos = (position % GRID).astype(jnp.float32)
    omega = 1.0 / 10000.0 ** (jnp.arange(half).astype(jnp.float32) / half)
    pieces = [
        jnp.repeat(coordinate[:, None] * omega[None, :], 2, axis=1)
        for coordinate in (frame, row_pos, col_pos)
    ]
    pieces.append(jnp.zeros((length, HD - 3 * section), jnp.float32))
    angles = jnp.concatenate(pieces, axis=1)
    parity = jnp.where(jnp.arange(HD) % 2 == 0, -1.0, 1.0).astype(jnp.float32)
    return (jnp.cos(angles), jnp.sin(angles) * parity)


def pair_swap(values):
    shape = values.shape
    paired = values.reshape(shape[:-1] + (shape[-1] // 2, 2))
    return paired[..., ::-1].reshape(shape)


def contract(left, right, left_dim, right_dim):
    return lax.dot_general(
        left, right, (((left_dim,), (right_dim,)), ((), ())), preferred_element_type=jnp.float32
    )


def exact_gelu(values):
    return jax.nn.gelu(values, approximate=False)


def body(
    activations,
    cotangent,
    attn_gain,
    attn_shift,
    qkv_weight,
    qkv_bias,
    out_weight,
    out_bias,
    mlp_gain,
    mlp_shift,
    fc1_weight,
    fc1_bias,
    fc2_weight,
    fc2_bias,
):
    tensor_size = lax.axis_size("tensor")
    tensor_rank = lax.axis_index("tensor")
    row_count = activations.shape[1]
    width = activations.shape[2]
    length = row_count * tensor_size
    block_rows = min(512, length)
    block_count = length // block_rows
    local_heads = qkv_weight.shape[1] // (3 * HD)
    packed_cols = qkv_weight.shape[1]
    unit_cols = fc1_weight.shape[1]
    factor = 1.0 / math.sqrt(HD)
    cosine, sine = rotary_tables(length)
    cosine = cosine[:, None, :]
    sine = sine[:, None, :]

    def rotate(values):
        return values * cosine + pair_swap(values) * sine

    def rotate_back(values):
        return values * cosine + pair_swap(values * sine)

    def fetch():
        gathered = (
            lax.all_gather(qkv_weight, "dp", axis=0, tiled=True),
            lax.all_gather(out_weight, "dp", axis=0, tiled=True),
            lax.all_gather(fc1_weight, "dp", axis=0, tiled=True),
            lax.all_gather(fc2_weight, "dp", axis=0, tiled=True),
        )
        return (gathered, gathered)

    def seq_gather(values):
        return lax.all_gather(values, "tensor", axis=0, tiled=True)

    def part_sum(values):
        return lax.psum_scatter(
            values.astype(jnp.bfloat16), "tensor", scatter_dimension=0, tiled=True
        ).astype(jnp.float32)

    def grad_gather(values):
        return lax.all_gather(values, "tensor", axis=0, tiled=True)

    def grad_sum(values):
        return lax.psum_scatter(
            values.astype(jnp.bfloat16), "tensor", scatter_dimension=0, tiled=True
        ).astype(jnp.float32)

    def forward(inputs, weights):
        (weight_qkv, weight_out, weight_up, weight_down), (
            whole_qkv,
            whole_out,
            whole_up,
            whole_down,
        ) = weights
        first_all = seq_gather(norm_rows(inputs, attn_gain, attn_shift).astype(jnp.bfloat16))
        packed = (
            jnp.dot(first_all, weight_qkv, preferred_element_type=jnp.float32) + qkv_bias
        ).reshape(length, local_heads, 3, HD)
        query = rotate(packed[:, :, 0]).astype(jnp.bfloat16)
        key_all = rotate(packed[:, :, 1]).astype(jnp.bfloat16)
        value_all = packed[:, :, 2].astype(jnp.bfloat16)
        outputs = []
        log_sums = []
        for block in range(block_count):
            query_block = query[block * block_rows : (block + 1) * block_rows]
            scores = (
                jnp.einsum("qhd,khd->hqk", query_block, key_all, preferred_element_type=jnp.float32)
                * factor
            )
            row_max = jnp.max(scores, axis=-1, keepdims=True)
            expo = jnp.exp(scores - row_max)
            row_total = jnp.sum(expo, axis=-1, keepdims=True)
            weights_low = (expo / row_total).astype(jnp.bfloat16)
            outputs.append(
                jnp.einsum(
                    "hqk,khd->qhd", weights_low, value_all, preferred_element_type=jnp.float32
                )
            )
            log_sums.append(row_max + jnp.log(row_total))
        heads_out = (
            jnp.concatenate(outputs, axis=0).reshape(length, local_heads * HD).astype(jnp.bfloat16)
        )
        log_total = jnp.concatenate(log_sums, axis=1)
        attended = part_sum(contract(heads_out, weight_out, 1, 1))
        resid = inputs + attended + out_bias
        second_all = seq_gather(norm_rows(resid, mlp_gain, mlp_shift).astype(jnp.bfloat16))
        hidden = jnp.dot(second_all, weight_up, preferred_element_type=jnp.float32) + fc1_bias
        act = exact_gelu(hidden).astype(jnp.bfloat16)
        branch = part_sum(contract(act, weight_down, 1, 1))
        result = resid + branch + fc2_bias
        kept = (
            first_all,
            query,
            key_all,
            value_all,
            log_total,
            heads_out,
            heads_out,
            resid,
            second_all,
            hidden,
            act,
        )
        return (result, kept)

    def backward(inputs, grad_low, kept, weights):
        (weight_qkv, weight_out, weight_up, weight_down), (
            whole_qkv,
            whole_out,
            whole_up,
            whole_down,
        ) = weights
        (
            first_all,
            query,
            key_all,
            value_all,
            log_total,
            heads_out,
            heads_rows,
            resid,
            second_all,
            hidden,
            act,
        ) = kept
        grad_top = grad_low.astype(jnp.float32)
        grad_fc2_bias = jnp.sum(grad_top, axis=0)
        grad_all = grad_gather(grad_low)
        grad_fc2_weight = contract(grad_all, act, 0, 0)
        grad_act = jnp.dot(grad_all, weight_down, preferred_element_type=jnp.float32)
        gelu_pull = jax.vjp(exact_gelu, hidden)[1]
        grad_hidden = gelu_pull(grad_act)[0].astype(jnp.bfloat16)
        grad_fc1_bias = jnp.sum(grad_hidden, axis=0, dtype=jnp.float32)
        grad_fc1_weight = contract(second_all, grad_hidden, 0, 0)
        grad_second = grad_sum(contract(grad_hidden, weight_up, 1, 1))
        second_pull = jax.vjp(norm_rows, resid, mlp_gain, mlp_shift)[1]
        grad_resid_norm, grad_mlp_gain, grad_mlp_shift = second_pull(grad_second)
        grad_resid = grad_top + grad_resid_norm
        grad_out_bias = jnp.sum(grad_resid, axis=0)
        resid_low = grad_resid.astype(jnp.bfloat16)
        resid_all = grad_gather(resid_low)
        grad_out_weight = contract(resid_all, heads_out, 0, 0)
        grad_heads = jnp.dot(resid_all, weight_out, preferred_element_type=jnp.float32).astype(
            jnp.bfloat16
        )
        grad_heads = grad_heads.reshape(length, local_heads, HD)
        grad_key = jnp.zeros((length, local_heads, HD), jnp.float32)
        grad_value = jnp.zeros((length, local_heads, HD), jnp.float32)
        query_grads = []
        for block in range(block_count):
            lower = block * block_rows
            upper = lower + block_rows
            query_block = query[lower:upper]
            grad_block = grad_heads[lower:upper]
            scores = (
                jnp.einsum("qhd,khd->hqk", query_block, key_all, preferred_element_type=jnp.float32)
                * factor
            )
            probs = jnp.exp(scores - log_total[:, lower:upper])
            grad_value = grad_value + jnp.einsum(
                "hqk,qhd->khd",
                probs.astype(jnp.bfloat16),
                grad_block,
                preferred_element_type=jnp.float32,
            )
            grad_probs = jnp.einsum(
                "qhd,khd->hqk", grad_block, value_all, preferred_element_type=jnp.float32
            )
            grad_scores = (
                probs * (grad_probs - jnp.sum(probs * grad_probs, axis=-1, keepdims=True))
            ).astype(jnp.bfloat16)
            query_grads.append(
                jnp.einsum("hqk,khd->qhd", grad_scores, key_all, preferred_element_type=jnp.float32)
                * factor
            )
            grad_key = (
                grad_key
                + jnp.einsum(
                    "hqk,qhd->khd", grad_scores, query_block, preferred_element_type=jnp.float32
                )
                * factor
            )
        grad_query = jnp.concatenate(query_grads, axis=0)
        grad_packed = jnp.stack(
            [rotate_back(grad_query), rotate_back(grad_key), grad_value], axis=2
        )
        grad_packed = grad_packed.reshape(length, packed_cols).astype(jnp.bfloat16)
        grad_qkv_bias = jnp.sum(grad_packed, axis=0, dtype=jnp.float32)
        grad_qkv_weight = contract(first_all, grad_packed, 0, 0)
        grad_first = grad_sum(contract(grad_packed, weight_qkv, 1, 1))
        first_pull = jax.vjp(norm_rows, inputs, attn_gain, attn_shift)[1]
        grad_input_norm, grad_attn_gain, grad_attn_shift = first_pull(grad_first)
        input_grad = grad_resid + grad_input_norm
        grads = (
            grad_attn_gain,
            grad_attn_shift,
            grad_qkv_weight,
            grad_qkv_bias,
            grad_out_weight,
            grad_out_bias,
            grad_mlp_gain,
            grad_mlp_shift,
            grad_fc1_weight,
            grad_fc1_bias,
            grad_fc2_weight,
            grad_fc2_bias,
        )
        return (input_grad, grads)

    def per_clip(totals, inputs_pair):
        clip_in, clip_grad = inputs_pair
        forward_weights = fetch()
        result, kept = forward(clip_in.astype(jnp.float32), forward_weights)
        backward_weights = fetch()
        input_grad, grads = backward(clip_in.astype(jnp.float32), clip_grad, kept, backward_weights)
        totals = tuple((left + right for left, right in zip(totals, grads)))
        return (totals, (result.astype(jnp.bfloat16), input_grad))

    out_cols = local_heads * HD
    start_totals = (
        jnp.zeros((width,), jnp.float32),
        jnp.zeros((width,), jnp.float32),
        jnp.zeros((width, packed_cols), jnp.float32),
        jnp.zeros((packed_cols,), jnp.float32),
        jnp.zeros((width, out_cols), jnp.float32),
        jnp.zeros((width,), jnp.float32),
        jnp.zeros((width,), jnp.float32),
        jnp.zeros((width,), jnp.float32),
        jnp.zeros((width, unit_cols), jnp.float32),
        jnp.zeros((unit_cols,), jnp.float32),
        jnp.zeros((width, unit_cols), jnp.float32),
        jnp.zeros((width,), jnp.float32),
    )
    totals, (output, input_grad) = lax.scan(per_clip, start_totals, (activations, cotangent))
    out_grad = totals[4]
    weight_sums = (
        lax.psum_scatter(
            totals[2].astype(jnp.bfloat16), "dp", scatter_dimension=0, tiled=True
        ).astype(jnp.float32),
        lax.psum_scatter(
            out_grad.astype(jnp.bfloat16), "dp", scatter_dimension=0, tiled=True
        ).astype(jnp.float32),
        lax.psum_scatter(
            totals[8].astype(jnp.bfloat16), "dp", scatter_dimension=0, tiled=True
        ).astype(jnp.float32),
        lax.psum_scatter(
            totals[10].astype(jnp.bfloat16), "dp", scatter_dimension=0, tiled=True
        ).astype(jnp.float32),
    )
    qkv_place = lax.dynamic_update_slice_in_dim(
        jnp.zeros((packed_cols * tensor_size,), jnp.float32),
        totals[3],
        tensor_rank * packed_cols,
        0,
    )
    unit_place = lax.dynamic_update_slice_in_dim(
        jnp.zeros((unit_cols * tensor_size,), jnp.float32), totals[9], tensor_rank * unit_cols, 0
    )
    summed = lax.psum(
        (totals[0], totals[1], qkv_place, totals[5], totals[6], totals[7], unit_place, totals[11]),
        ("dp", "tensor"),
    )
    grad_qkv_bias = lax.dynamic_slice_in_dim(summed[2], tensor_rank * packed_cols, packed_cols, 0)
    grad_fc1_bias = lax.dynamic_slice_in_dim(summed[6], tensor_rank * unit_cols, unit_cols, 0)
    return (
        output,
        input_grad,
        summed[0],
        summed[1],
        weight_sums[0],
        grad_qkv_bias,
        weight_sums[1],
        summed[3],
        summed[4],
        summed[5],
        weight_sums[2],
        grad_fc1_bias,
        weight_sums[3],
        summed[7],
    )


def solution(mesh):
    in_specs = (
        P("dp", "tensor", None),
        P("dp", "tensor", None),
        P(),
        P(),
        P("dp", "tensor"),
        P("tensor"),
        P("dp", "tensor"),
        P(),
        P(),
        P(),
        P("dp", "tensor"),
        P("tensor"),
        P("dp", "tensor"),
        P(),
    )
    out_specs = (
        P("dp", "tensor", None),
        P("dp", "tensor", None),
        P(),
        P(),
        P("dp", "tensor"),
        P("tensor"),
        P("dp", "tensor"),
        P(),
        P(),
        P(),
        P("dp", "tensor"),
        P("tensor"),
        P("dp", "tensor"),
        P(),
    )
    return jax.shard_map(body, mesh=mesh, in_specs=in_specs, out_specs=out_specs, check_vma=False)
```

profile of v0, /device:TPU:0, one launch (start us, length us, event | category | flops | bytes accessed | tf_op | source)
XLA Modules:
  0.0 1281.7 jit_solution(289971395987647129)
XLA Ops:
  12.3 1092.1 %while.38 = (s32[]{:T(128)}, f32[1024]{0:T(1024)}, f32[1024]{0:T(1024)}, f32[1024,768]{1,0:T(8,128)}, f32[768]{0:T(1024)}, /*index=5*/f32[1024,256]{1,0:T(8,128)...) while((s32[]{:T(128)}, f32[1024]{0:T(1024)}, ...), condition=%wide.wide.region_27.28_spmd.clone, body=%wide.wide.region_0.27_spmd.clone.sunk | while | flops 22775205888 | bytes 743322112 | solution.py:300
  17.9 14.5 %all_gather.51 = bf16[1024,256]{1,0:T(8,128)(2,1)} all-gather(bf16[128,256]{1,0:T(8,128)(2,1)} %get-tuple-element.931), channel_id=1, replica_groups=mesh['dp'=8,'tensor'=4] {'dp'}, dimensions={0}, use_global_device_ids=true | all-gather | bytes 589824 | tf_op jit(solution)/shard_map/while/body/eval_jaxpr/all_gather | solution.py:92
  32.4 12.2 all-gather.15.cloned.1.call-done
  44.7 47.8 %all-gather.13.cloned.1.call-done = bf16[1024,1024]{1,0:T(8,128)(2,1)} async-done(((bf16[256,1024]{1,0:T(8,128)(2,1)}), bf16[1024,1024]{1,0:T(8,128)(2,1)}) %all-gather.13.cloned.1.call-update) | async-done | bytes 2097168 | tf_op jit(solution)/shard_map/while/body/eval_jaxpr/all_gather | solution.py:99
  92.5 3.9 convolution_add_fusion.7
  99.9 5.3 rev.25
  108.5 5.2 rev.24
  134.9 42.0 %reduce-scatter.17.cloned.1.call-done = bf16[256,1024]{1,0:T(8,128)(2,1)} async-done(((bf16[1024,1024]{1,0:T(8,128)(2,1)}), bf16[256,1024]{1,0:T(8,128)(2,1)}) %reduce-scatter.17.cloned.1.call-update) | async-done | bytes 524304 | tf_op jit(solution)/shard_map/while/body/eval_jaxpr/reduce_scatter | solution.py:102
  183.5 22.1 %all-gather.19.cloned.1.call-done = bf16[1024,1024]{1,0:T(8,128)(2,1)} async-done(((bf16[128,1024]{1,0:T(8,128)(2,1)}), bf16[1024,1024]{1,0:T(8,128)(2,1)}) %all-gather.19.cloned.1.call-update) | async-done | bytes 2097168 | tf_op jit(solution)/shard_map/while/body/eval_jaxpr/all_gather | solution.py:93
  205.6 47.7 %all-gather.17.cloned.1.call-done = bf16[1024,1024]{1,0:T(8,128)(2,1)} async-done(((bf16[256,1024]{1,0:T(8,128)(2,1)}), bf16[1024,1024]{1,0:T(8,128)(2,1)}) %all-gather.17.cloned.1.call-update) | async-done | bytes 2097168 | tf_op jit(solution)/shard_map/while/body/eval_jaxpr/all_gather | solution.py:99
  253.2 15.4 %multiply_convert_fusion.9 = (bf16[1024,1024]{1,0:T(8,128)(2,1)}, f32[1024,1024]{1,0:T(8,128)}, f32[1024,1024]{1,0:T(8,128)}) fusion(f32[1024]{0:T(1024)S(1)} %copy-done.66, bf16[1024,1024]{1,0:T(8,128)(2,1)} %all-gather.17.cloned.1.call-done, bf16[1024,1024]{1,0:T(8,128)(2,1)} %all-gather.19.cloned.1.call-done), kind=kOutput, calls=%fused_computation.22.clone.clone.1 | convolution fusion | flops 2216689664 | bytes 14684160 | tf_op jit(solution)/shard_map/while/body/eval_jaxpr/dot_general | solution.py:153
  268.6 31.1 %all-gather.23.cloned.1.call-done = bf16[1,1024,1024]{2,1,0:T(8,128)(2,1)} async-done(((bf16[1,256,1024]{2,1,0:T(8,128)(2,1)}), bf16[1,1024,1024]{2,1,0:T(8,128)(2,1)}) %all-gather.23.cloned.1.call-update) | async-done | bytes 2097168 | tf_op jit(solution)/shard_map/while/body/eval_jaxpr/all_gather | solution.py:107
  299.7 28.5 %all-gather.21.cloned.1.call-done = bf16[1024,1024]{1,0:T(8,128)(2,1)} async-done(((bf16[128,1024]{1,0:T(8,128)(2,1)}), bf16[1024,1024]{1,0:T(8,128)(2,1)}) %all-gather.21.cloned.1.call-update) | async-done | bytes 2097168 | tf_op jit(solution)/shard_map/while/body/eval_jaxpr/all_gather | solution.py:94
  328.2 8.4 convert_reduce_fusion.18
  338.0 3.7 convolution_convert_fusion.16
  341.8 43.7 %reduce-scatter.19.cloned.1.call-done = bf16[256,1024]{1,0:T(8,128)(2,1)} async-done(((bf16[1024,1024]{1,0:T(8,128)(2,1)}), bf16[256,1024]{1,0:T(8,128)(2,1)}) %reduce-scatter.19.cloned.1.call-update) | async-done | bytes 524304 | tf_op jit(solution)/shard_map/while/body/eval_jaxpr/reduce_scatter | solution.py:110
  394.1 6.0 convolution_convert_fusion.19
  400.4 36.9 %all-gather.25.cloned.1.call-done = bf16[1024,1024]{1,0:T(8,128)(2,1)} async-done(((bf16[256,1024]{1,0:T(8,128)(2,1)}), bf16[1024,1024]{1,0:T(8,128)(2,1)}) %all-gather.25.cloned.1.call-update) | async-done | bytes 2097168 | tf_op jit(solution)/shard_map/while/body/eval_jaxpr/all_gather | solution.py:107
  440.3 5.4 multiply_reduce_fusion.18
  451.0 6.1 multiply_reduce_fusion.19
  459.6 7.0 multiply_convert_fusion.11
  472.7 4.1 rev.26
  479.9 3.6 convolution_multiply_fusion.6
  486.3 6.3 rev.27
  499.0 4.5 fusion.336
  510.6 6.2 select_add_fusion.37
  516.9 4.4 select_add_fusion.39
  526.7 3.5 select_add_fusion.33
  530.2 22.9 %reduce-scatter.21.cloned.1.call-done = bf16[256,1024]{1,0:T(8,128)(2,1)} async-done(((bf16[1024,1024]{1,0:T(8,128)(2,1)}), bf16[256,1024]{1,0:T(8,128)(2,1)}) %reduce-scatter.21.cloned.1.call-update) | async-done | bytes 524304 | tf_op jit(solution)/shard_map/while/body/eval_jaxpr/reduce_scatter | solution.py:110
  564.5 11.8 all_gather.51
  576.4 11.2 all-gather.15.cloned.1.call-done
  587.6 47.8 %all-gather.13.cloned.1.call-done = bf16[1024,1024]{1,0:T(8,128)(2,1)} async-done(((bf16[256,1024]{1,0:T(8,128)(2,1)}), bf16[1024,1024]{1,0:T(8,128)(2,1)}) %all-gather.13.cloned.1.call-update) | async-done | bytes 2097168 | tf_op jit(solution)/shard_map/while/body/eval_jaxpr/all_gather | solution.py:99
  635.4 3.9 convolution_add_fusion.7
  642.8 5.3 rev.25
  651.5 5.2 rev.24
  677.8 41.9 %reduce-scatter.17.cloned.1.call-done = bf16[256,1024]{1,0:T(8,128)(2,1)} async-done(((bf16[1024,1024]{1,0:T(8,128)(2,1)}), bf16[256,1024]{1,0:T(8,128)(2,1)}) %reduce-scatter.17.cloned.1.call-update) | async-done | bytes 524304 | tf_op jit(solution)/shard_map/while/body/eval_jaxpr/reduce_scatter | solution.py:102
  726.2 22.3 %all-gather.19.cloned.1.call-done = bf16[1024,1024]{1,0:T(8,128)(2,1)} async-done(((bf16[128,1024]{1,0:T(8,128)(2,1)}), bf16[1024,1024]{1,0:T(8,128)(2,1)}) %all-gather.19.cloned.1.call-update) | async-done | bytes 2097168 | tf_op jit(solution)/shard_map/while/body/eval_jaxpr/all_gather | solution.py:93
  748.5 47.7 %all-gather.17.cloned.1.call-done = bf16[1024,1024]{1,0:T(8,128)(2,1)} async-done(((bf16[256,1024]{1,0:T(8,128)(2,1)}), bf16[1024,1024]{1,0:T(8,128)(2,1)}) %all-gather.17.cloned.1.call-update) | async-done | bytes 2097168 | tf_op jit(solution)/shard_map/while/body/eval_jaxpr/all_gather | solution.py:99
  796.2 15.4 %multiply_convert_fusion.9 = (bf16[1024,1024]{1,0:T(8,128)(2,1)}, f32[1024,1024]{1,0:T(8,128)}, f32[1024,1024]{1,0:T(8,128)}) fusion(f32[1024]{0:T(1024)S(1)} %copy-done.66, bf16[1024,1024]{1,0:T(8,128)(2,1)} %all-gather.17.cloned.1.call-done, bf16[1024,1024]{1,0:T(8,128)(2,1)} %all-gather.19.cloned.1.call-done), kind=kOutput, calls=%fused_computation.22.clone.clone.1 | convolution fusion | flops 2216689664 | bytes 14684160 | tf_op jit(solution)/shard_map/while/body/eval_jaxpr/dot_general | solution.py:153
  811.6 31.1 %all-gather.23.cloned.1.call-done = bf16[1,1024,1024]{2,1,0:T(8,128)(2,1)} async-done(((bf16[1,256,1024]{2,1,0:T(8,128)(2,1)}), bf16[1,1024,1024]{2,1,0:T(8,128)(2,1)}) %all-gather.23.cloned.1.call-update) | async-done | bytes 2097168 | tf_op jit(solution)/shard_map/while/body/eval_jaxpr/all_gather | solution.py:107
  842.7 28.4 %all-gather.21.cloned.1.call-done = bf16[1024,1024]{1,0:T(8,128)(2,1)} async-done(((bf16[128,1024]{1,0:T(8,128)(2,1)}), bf16[1024,1024]{1,0:T(8,128)(2,1)}) %all-gather.21.cloned.1.call-update) | async-done | bytes 2097168 | tf_op jit(solution)/shard_map/while/body/eval_jaxpr/all_gather | solution.py:94
  871.0 8.4 convert_reduce_fusion.18
  880.8 3.7 convolution_convert_fusion.16
  884.6 43.7 %reduce-scatter.19.cloned.1.call-done = bf16[256,1024]{1,0:T(8,128)(2,1)} async-done(((bf16[1024,1024]{1,0:T(8,128)(2,1)}), bf16[256,1024]{1,0:T(8,128)(2,1)}) %reduce-scatter.19.cloned.1.call-update) | async-done | bytes 524304 | tf_op jit(solution)/shard_map/while/body/eval_jaxpr/reduce_scatter | solution.py:110
  936.9 6.0 convolution_convert_fusion.19
  943.2 36.9 %all-gather.25.cloned.1.call-done = bf16[1024,1024]{1,0:T(8,128)(2,1)} async-done(((bf16[256,1024]{1,0:T(8,128)(2,1)}), bf16[1024,1024]{1,0:T(8,128)(2,1)}) %all-gather.25.cloned.1.call-update) | async-done | bytes 2097168 | tf_op jit(solution)/shard_map/while/body/eval_jaxpr/all_gather | solution.py:107
  983.1 5.4 multiply_reduce_fusion.18
  993.8 6.1 multiply_reduce_fusion.19
  1002.5 7.0 multiply_convert_fusion.11
  1015.5 4.1 rev.26
  1022.7 3.6 convolution_multiply_fusion.6
  1029.1 6.3 rev.27
  1041.8 4.5 fusion.336
  1053.4 7.4 select_add_fusion.37
  1060.9 6.7 select_add_fusion.39
  1073.1 5.8 select_add_fusion.33
  1078.9 17.0 %reduce-scatter.21.cloned.1.call-done = bf16[256,1024]{1,0:T(8,128)(2,1)} async-done(((bf16[1024,1024]{1,0:T(8,128)(2,1)}), bf16[256,1024]{1,0:T(8,128)(2,1)}) %reduce-scatter.21.cloned.1.call-update) | async-done | bytes 524304 | tf_op jit(solution)/shard_map/while/body/eval_jaxpr/reduce_scatter | solution.py:110
  1106.7 3.2 convert_element_type.161
  1110.0 3.9 convert_element_type.165
  1114.0 4.0 convert_element_type.167
  1118.6 40.9 %all-reduce = (f32[1024]{0:T(1024)}, f32[1024]{0:T(1024)}, f32[3072]{0:T(1024)S(1)}, f32[1024]{0:T(1024)}, f32[1024]{0:T(1024)}, /*index=5*/f32[1024]{0:T(1024)}, f32[4096]{0:T(1024)S(1)}, f32[1024]{0:T(1024)}) all-reduce(f32[1024]{0:T(1024)S(1)} %copy-done.58, ...), channel_id=1, replica_groups=mesh['dp'=8,'tensor'=4] {'dp','tensor'}, use_global_device_ids=true, to_apply=%region_28.29 | all-reduce | flops 13312 | bytes 106496 | tf_op jit(solution)/shard_map/psum | solution.py:325
  1162.3 21.2 %reduce-scatter.9.cloned.1.call-done = bf16[128,768]{1,0:T(8,128)(2,1)} async-done(((bf16[1024,768]{1,0:T(8,128)(2,1)}), bf16[128,768]{1,0:T(8,128)(2,1)}) %reduce-scatter.9.cloned.1.call-update) | async-done | bytes 196624 | tf_op jit(solution)/shard_map/reduce_scatter | solution.py:303
  1185.1 42.5 %reduce-scatter.13.cloned.1.call-done = bf16[128,1024]{1,0:T(8,128)(2,1)} async-done(((bf16[1024,1024]{1,0:T(8,128)(2,1)}), bf16[128,1024]{1,0:T(8,128)(2,1)}) %reduce-scatter.13.cloned.1.call-update) | async-done | bytes 262160 | tf_op jit(solution)/shard_map/reduce_scatter | solution.py:309
  1229.4 42.5 %reduce-scatter.15.cloned.1.call-done = bf16[128,1024]{1,0:T(8,128)(2,1)} async-done(((bf16[1024,1024]{1,0:T(8,128)(2,1)}), bf16[128,1024]{1,0:T(8,128)(2,1)}) %reduce-scatter.15.cloned.1.call-update) | async-done | bytes 262160 | tf_op jit(solution)/shard_map/reduce_scatter | solution.py:312
  (525 shorter events, 208.0 us)
Async XLA Ops:
  12.3 380.0 %copy-start.19 = (f32[1024,1,64]{0,2,1:T(8,128)}, f32[1024,1,64]{0,2,1:T(8,128)S(1)}, u32[]{:S(2)}) copy-start(f32[1024,1,64]{0,2,1:T(8,128)S(1)} %get-tuple-element.928) | copy-start | bytes 786436 | tf_op jit(solution)/shard_map/while
  12.3 32.3 %all-gather.15.cloned.1.call-start = ((), (), s32[]{:S(2)}) async-start(), calls=%async_computation.13 | async-start | bytes 1769472 | tf_op jit(solution)/shard_map/while/body/eval_jaxpr/all_gather | solution.py:91
  13.0 79.4 %all-gather.13.cloned.1.call-start = ((), (), s32[]{:S(2)}) async-start(), calls=%async_computation.12 | async-start | bytes 2621440 | tf_op jit(solution)/shard_map/while/body/eval_jaxpr/all_gather | solution.py:99
  14.3 82.1 %copy-start.35 = (f32[256]{0:T(256)}, f32[256]{0:T(256)S(1)}, u32[]{:S(2)}) copy-start(f32[256]{0:T(256)S(1)} %broadcast_multiply_fusion.16) | copy-start | bytes 3076 | tf_op jit(solution)/shard_map/while
  15.6 80.8 %copy-start.39 = (f32[256]{0:T(256)}, f32[256]{0:T(256)S(1)}, u32[]{:S(2)}) copy-start(f32[256]{0:T(256)S(1)} %fusion.322) | copy-start | bytes 3076 | tf_op jit(solution)/shard_map/while
  15.7 80.8 %copy-start.37 = (f32[256]{0:T(256)}, f32[256]{0:T(256)S(1)}, u32[]{:S(2)}) copy-start(f32[256]{0:T(256)S(1)} %fusion.323) | copy-start | bytes 3076 | tf_op jit(solution)/shard_map/while
  17.8 159.0 %reduce-scatter.17.cloned.1.call-start = ((), (), s32[]{:S(2)}) async-start(), calls=%async_computation.14 | async-start | bytes 2621440 | tf_op jit(solution)/shard_map/while/body/eval_jaxpr/reduce_scatter | solution.py:102
  131.2 45.6 %copy-start.2 = (bf16[2,256,1024]{2,1,0:T(8,128)(2,1)S(1)}, bf16[2,256,1024]{2,1,0:T(8,128)(2,1)}, u32[]{:S(2)}) copy-start(bf16[2,256,1024]{2,1,0:T(8,128)(2,1)} %get-tuple-element.923) | copy-start | bytes 3145732 | tf_op jit(solution)/shard_map/while
  131.2 45.6 %copy-start.32 = (f32[1024]{0:T(1024)S(1)}, f32[1024]{0:T(1024)}, u32[]{:S(2)}) copy-start(f32[1024]{0:T(1024)} %get-tuple-element.932) | copy-start | bytes 12292 | tf_op jit(solution)/shard_map/while
  131.2 48.3 %copy-start.34 = (f32[1024]{0:T(1024)S(1)}, f32[1024]{0:T(1024)}, u32[]{:S(2)}) copy-start(f32[1024]{0:T(1024)} %get-tuple-element.933) | copy-start | bytes 12292 | tf_op jit(solution)/shard_map/while
  131.2 48.3 %copy-start.59 = (f32[1024]{0:T(1024)S(1)}, f32[1024]{0:T(1024)}, u32[]{:S(2)}) copy-start(f32[1024]{0:T(1024)} %get-tuple-element.934) | copy-start | bytes 12292 | tf_op jit(solution)/shard_map/while
  132.1 49.7 %copy-start.31 = (bf16[2,256,1024]{2,1,0:T(8,128)(2,1)S(1)}, bf16[2,256,1024]{2,1,0:T(8,128)(2,1)}, u32[]{:S(2)}) copy-start(bf16[2,256,1024]{2,1,0:T(8,128)(2,1)} %get-tuple-element.930) | copy-start | bytes 3145732 | tf_op jit(solution)/shard_map/while
  134.2 119.0 %copy-start.66 = (f32[1024]{0:T(1024)S(1)}, f32[1024]{0:T(1024)}, u32[]{:S(2)}) copy-start(f32[1024]{0:T(1024)} %get-tuple-element.936) | copy-start | bytes 12292 | tf_op jit(solution)/shard_map/while
  134.2 71.3 %all-gather.19.cloned.1.call-start = ((), (), s32[]{:S(2)}) async-start(), calls=%async_computation.16 | async-start | bytes 2359296 | tf_op jit(solution)/shard_map/while/body/eval_jaxpr/all_gather | solution.py:93
  134.8 118.4 %all-gather.17.cloned.1.call-start = ((), (), s32[]{:S(2)}) async-start(), calls=%async_computation.15 | async-start | bytes 2621440 | tf_op jit(solution)/shard_map/while/body/eval_jaxpr/all_gather | solution.py:99
  181.7 118.0 %all-gather.23.cloned.1.call-start = ((), (), s32[]{:S(2)}) async-start(), calls=%async_computation.18 | async-start | bytes 2621440 | tf_op jit(solution)/shard_map/while/body/eval_jaxpr/all_gather | solution.py:107
  182.7 145.6 %all-gather.21.cloned.1.call-start = ((), (), s32[]{:S(2)}) async-start(), calls=%async_computation.17 | async-start | bytes 2359296 | tf_op jit(solution)/shard_map/while/body/eval_jaxpr/all_gather | solution.py:94
  183.4 202.1 %reduce-scatter.19.cloned.1.call-start = ((), (), s32[]{:S(2)}) async-start(), calls=%async_computation.19 | async-start | bytes 2621440 | tf_op jit(solution)/shard_map/while/body/eval_jaxpr/reduce_scatter | solution.py:110
  338.0 47.5 %copy-start.4 = (bf16[256,1024]{1,0:T(8,128)(2,1)S(1)}, bf16[256,1024]{1,0:T(8,128)(2,1)}, u32[]{:S(2)}) copy-start(bf16[256,1024]{1,0:T(8,128)(2,1)} %reduce-scatter.17.cloned.1.call-done) | copy-start | bytes 1572868 | tf_op jit(solution)/shard_map/while
  341.7 47.1 %copy-start.14 = (bf16[1,256,1024]{2,1,0:T(8,128)(2,1)S(1)}, bf16[1,256,1024]{2,1,0:T(8,128)(2,1)}, u32[]{:S(2)}) copy-start(bf16[1,256,1024]{2,1,0:T(8,128)(2,1)} %get-tuple-element.811) | copy-start | bytes 1572868 | tf_op jit(solution)/shard_map/while
  341.7 95.5 %all-gather.25.cloned.1.call-start = ((), (), s32[]{:S(2)}) async-start(), calls=%async_computation.20 | async-start | bytes 2621440 | tf_op jit(solution)/shard_map/while/body/eval_jaxpr/all_gather | solution.py:107
  392.2 129.1 %reduce-scatter.23.cloned.1.call-start = ((), (), s32[]{:S(2)}) async-start(), calls=%async_computation.22 | async-start | bytes 2621440 | tf_op jit(solution)/shard_map/while/body/eval_jaxpr/reduce_scatter | solution.py:102
  400.1 153.0 %reduce-scatter.21.cloned.1.call-start = ((), (), s32[]{:S(2)}) async-start(), calls=%async_computation.21 | async-start | bytes 2621440 | tf_op jit(solution)/shard_map/while/body/eval_jaxpr/reduce_scatter | solution.py:110
  526.6 26.5 %copy-start.33 = (f32[1024]{0:T(1024)S(1)}, f32[1024]{0:T(1024)}, u32[]{:S(2)}) copy-start(f32[1024]{0:T(1024)} %get-tuple-element.924) | copy-start | bytes 12292 | tf_op jit(solution)/shard_map/while
  526.6 26.5 %copy-start.36 = (f32[256]{0:T(256)S(1)}, f32[256]{0:T(256)}, u32[]{:S(2)}) copy-start(f32[256]{0:T(256)} %copy-done.35) | copy-start | bytes 3076 | tf_op jit(solution)/shard_map/while
  526.6 27.9 %copy-start.40 = (f32[256]{0:T(256)S(1)}, f32[256]{0:T(256)}, u32[]{:S(2)}) copy-start(f32[256]{0:T(256)} %copy-done.39) | copy-start | bytes 3076 | tf_op jit(solution)/shard_map/while
  526.6 27.9 %copy-start.38 = (f32[256]{0:T(256)S(1)}, f32[256]{0:T(256)}, u32[]{:S(2)}) copy-start(f32[256]{0:T(256)} %copy-done.37) | copy-start | bytes 3076 | tf_op jit(solution)/shard_map/while
  526.6 29.5 %copy-start.56 = (f32[1024]{0:T(1024)S(1)}, f32[1024]{0:T(1024)}, u32[]{:S(2)}) copy-start(f32[1024]{0:T(1024)} %get-tuple-element.875) | copy-start | bytes 12292 | tf_op jit(solution)/shard_map/while
  526.6 29.5 %copy-start.53 = (f32[1024]{0:T(1024)S(1)}, f32[1024]{0:T(1024)}, u32[]{:S(2)}) copy-start(f32[1024]{0:T(1024)} %get-tuple-element.876) | copy-start | bytes 12292 | tf_op jit(solution)/shard_map/while
  526.7 29.6 %copy-start.9 = (f32[256,1024]{1,0:T(8,128)S(1)}, f32[256,1024]{1,0:T(8,128)}, u32[]{:S(2)}) copy-start(f32[256,1024]{1,0:T(8,128)} %copy-done.8) | copy-start | bytes 3145732 | tf_op jit(solution)/shard_map/while
  559.1 376.0 %copy-start.19 = (f32[1024,1,64]{0,2,1:T(8,128)}, f32[1024,1,64]{0,2,1:T(8,128)S(1)}, u32[]{:S(2)}) copy-start(f32[1024,1,64]{0,2,1:T(8,128)S(1)} %get-tuple-element.928) | copy-start | bytes 786436 | tf_op jit(solution)/shard_map/while
  559.1 28.5 %all-gather.15.cloned.1.call-start = ((), (), s32[]{:S(2)}) async-start(), calls=%async_computation.13 | async-start | bytes 1769472 | tf_op jit(solution)/shard_map/while/body/eval_jaxpr/all_gather | solution.py:91
  559.7 75.7 %all-gather.13.cloned.1.call-start = ((), (), s32[]{:S(2)}) async-start(), calls=%async_computation.12 | async-start | bytes 2621440 | tf_op jit(solution)/shard_map/while/body/eval_jaxpr/all_gather | solution.py:99
  560.9 78.4 %copy-start.35 = (f32[256]{0:T(256)}, f32[256]{0:T(256)S(1)}, u32[]{:S(2)}) copy-start(f32[256]{0:T(256)S(1)} %broadcast_multiply_fusion.16) | copy-start | bytes 3076 | tf_op jit(solution)/shard_map/while
  562.3 77.1 %copy-start.39 = (f32[256]{0:T(256)}, f32[256]{0:T(256)S(1)}, u32[]{:S(2)}) copy-start(f32[256]{0:T(256)S(1)} %fusion.322) | copy-start | bytes 3076 | tf_op jit(solution)/shard_map/while
  562.3 77.1 %copy-start.37 = (f32[256]{0:T(256)}, f32[256]{0:T(256)S(1)}, u32[]{:S(2)}) copy-start(f32[256]{0:T(256)S(1)} %fusion.323) | copy-start | bytes 3076 | tf_op jit(solution)/shard_map/while
  564.5 155.3 %reduce-scatter.17.cloned.1.call-start = ((), (), s32[]{:S(2)}) async-start(), calls=%async_computation.14 | async-start | bytes 2621440 | tf_op jit(solution)/shard_map/while/body/eval_jaxpr/reduce_scatter | solution.py:102
  674.1 45.6 %copy-start.2 = (bf16[2,256,1024]{2,1,0:T(8,128)(2,1)S(1)}, bf16[2,256,1024]{2,1,0:T(8,128)(2,1)}, u32[]{:S(2)}) copy-start(bf16[2,256,1024]{2,1,0:T(8,128)(2,1)} %get-tuple-element.923) | copy-start | bytes 3145732 | tf_op jit(solution)/shard_map/while
  674.1 45.6 %copy-start.32 = (f32[1024]{0:T(1024)S(1)}, f32[1024]{0:T(1024)}, u32[]{:S(2)}) copy-start(f32[1024]{0:T(1024)} %get-tuple-element.932) | copy-start | bytes 12292 | tf_op jit(solution)/shard_map/while
  674.1 48.3 %copy-start.34 = (f32[1024]{0:T(1024)S(1)}, f32[1024]{0:T(1024)}, u32[]{:S(2)}) copy-start(f32[1024]{0:T(1024)} %get-tuple-element.933) | copy-start | bytes 12292 | tf_op jit(solution)/shard_map/while
  674.1 48.3 %copy-start.59 = (f32[1024]{0:T(1024)S(1)}, f32[1024]{0:T(1024)}, u32[]{:S(2)}) copy-start(f32[1024]{0:T(1024)} %get-tuple-element.934) | copy-start | bytes 12292 | tf_op jit(solution)/shard_map/while
  675.0 49.7 %copy-start.31 = (bf16[2,256,1024]{2,1,0:T(8,128)(2,1)S(1)}, bf16[2,256,1024]{2,1,0:T(8,128)(2,1)}, u32[]{:S(2)}) copy-start(bf16[2,256,1024]{2,1,0:T(8,128)(2,1)} %get-tuple-element.930) | copy-start | bytes 3145732 | tf_op jit(solution)/shard_map/while
  677.1 119.1 %copy-start.66 = (f32[1024]{0:T(1024)S(1)}, f32[1024]{0:T(1024)}, u32[]{:S(2)}) copy-start(f32[1024]{0:T(1024)} %get-tuple-element.936) | copy-start | bytes 12292 | tf_op jit(solution)/shard_map/while
  677.2 71.3 %all-gather.19.cloned.1.call-start = ((), (), s32[]{:S(2)}) async-start(), calls=%async_computation.16 | async-start | bytes 2359296 | tf_op jit(solution)/shard_map/while/body/eval_jaxpr/all_gather | solution.py:93
  677.8 118.4 %all-gather.17.cloned.1.call-start = ((), (), s32[]{:S(2)}) async-start(), calls=%async_computation.15 | async-start | bytes 2621440 | tf_op jit(solution)/shard_map/while/body/eval_jaxpr/all_gather | solution.py:99
  724.7 118.0 %all-gather.23.cloned.1.call-start = ((), (), s32[]{:S(2)}) async-start(), calls=%async_computation.18 | async-start | bytes 2621440 | tf_op jit(solution)/shard_map/while/body/eval_jaxpr/all_gather | solution.py:107
  725.6 145.4 %all-gather.21.cloned.1.call-start = ((), (), s32[]{:S(2)}) async-start(), calls=%async_computation.17 | async-start | bytes 2359296 | tf_op jit(solution)/shard_map/while/body/eval_jaxpr/all_gather | solution.py:94
  726.2 202.1 %reduce-scatter.19.cloned.1.call-start = ((), (), s32[]{:S(2)}) async-start(), calls=%async_computation.19 | async-start | bytes 2621440 | tf_op jit(solution)/shard_map/while/body/eval_jaxpr/reduce_scatter | solution.py:110
  880.8 47.5 %copy-start.4 = (bf16[256,1024]{1,0:T(8,128)(2,1)S(1)}, bf16[256,1024]{1,0:T(8,128)(2,1)}, u32[]{:S(2)}) copy-start(bf16[256,1024]{1,0:T(8,128)(2,1)} %reduce-scatter.17.cloned.1.call-done) | copy-start | bytes 1572868 | tf_op jit(solution)/shard_map/while
  884.5 47.1 %copy-start.14 = (bf16[1,256,1024]{2,1,0:T(8,128)(2,1)S(1)}, bf16[1,256,1024]{2,1,0:T(8,128)(2,1)}, u32[]{:S(2)}) copy-start(bf16[1,256,1024]{2,1,0:T(8,128)(2,1)} %get-tuple-element.811) | copy-start | bytes 1572868 | tf_op jit(solution)/shard_map/while
  884.5 95.5 %all-gather.25.cloned.1.call-start = ((), (), s32[]{:S(2)}) async-start(), calls=%async_computation.20 | async-start | bytes 2621440 | tf_op jit(solution)/shard_map/while/body/eval_jaxpr/all_gather | solution.py:107
  935.0 132.7 %reduce-scatter.23.cloned.1.call-start = ((), (), s32[]{:S(2)}) async-start(), calls=%async_computation.22 | async-start | bytes 2621440 | tf_op jit(solution)/shard_map/while/body/eval_jaxpr/reduce_scatter | solution.py:102
  942.9 153.0 %reduce-scatter.21.cloned.1.call-start = ((), (), s32[]{:S(2)}) async-start(), calls=%async_computation.21 | async-start | bytes 2621440 | tf_op jit(solution)/shard_map/while/body/eval_jaxpr/reduce_scatter | solution.py:110
  1073.0 22.9 %copy-start.33 = (f32[1024]{0:T(1024)S(1)}, f32[1024]{0:T(1024)}, u32[]{:S(2)}) copy-start(f32[1024]{0:T(1024)} %get-tuple-element.924) | copy-start | bytes 12292 | tf_op jit(solution)/shard_map/while
  1073.0 22.9 %copy-start.36 = (f32[256]{0:T(256)S(1)}, f32[256]{0:T(256)}, u32[]{:S(2)}) copy-start(f32[256]{0:T(256)} %copy-done.35) | copy-start | bytes 3076 | tf_op jit(solution)/shard_map/while
  1073.0 24.3 %copy-start.40 = (f32[256]{0:T(256)S(1)}, f32[256]{0:T(256)}, u32[]{:S(2)}) copy-start(f32[256]{0:T(256)} %copy-done.39) | copy-start | bytes 3076 | tf_op jit(solution)/shard_map/while
  1073.0 24.3 %copy-start.38 = (f32[256]{0:T(256)S(1)}, f32[256]{0:T(256)}, u32[]{:S(2)}) copy-start(f32[256]{0:T(256)} %copy-done.37) | copy-start | bytes 3076 | tf_op jit(solution)/shard_map/while
  1073.0 25.9 %copy-start.56 = (f32[1024]{0:T(1024)S(1)}, f32[1024]{0:T(1024)}, u32[]{:S(2)}) copy-start(f32[1024]{0:T(1024)} %get-tuple-element.875) | copy-start | bytes 12292 | tf_op jit(solution)/shard_map/while
  1073.0 25.9 %copy-start.53 = (f32[1024]{0:T(1024)S(1)}, f32[1024]{0:T(1024)}, u32[]{:S(2)}) copy-start(f32[1024]{0:T(1024)} %get-tuple-element.876) | copy-start | bytes 12292 | tf_op jit(solution)/shard_map/while
  1073.1 26.0 %copy-start.9 = (f32[256,1024]{1,0:T(8,128)S(1)}, f32[256,1024]{1,0:T(8,128)}, u32[]{:S(2)}) copy-start(f32[256,1024]{1,0:T(8,128)} %copy-done.8) | copy-start | bytes 3145732 | tf_op jit(solution)/shard_map/while
  1104.5 56.3 %reduce-scatter.11.cloned.1.call-start = ((), (), s32[]{:S(2)}) async-start(), calls=%async_computation.9 | async-start | bytes 589824 | tf_op jit(solution)/shard_map/reduce_scatter | solution.py:306
  1106.6 76.8 %reduce-scatter.9.cloned.1.call-start = ((), (), s32[]{:S(2)}) async-start(), calls=%async_computation.8 | async-start | bytes 1769472 | tf_op jit(solution)/shard_map/reduce_scatter | solution.py:303
  1109.9 117.7 %reduce-scatter.13.cloned.1.call-start = ((), (), s32[]{:S(2)}) async-start(), calls=%async_computation.10 | async-start | bytes 2359296 | tf_op jit(solution)/shard_map/reduce_scatter | solution.py:309
  1113.8 158.1 %reduce-scatter.15.cloned.1.call-start = ((), (), s32[]{:S(2)}) async-start(), calls=%async_computation.11 | async-start | bytes 2359296 | tf_op jit(solution)/shard_map/reduce_scatter | solution.py:312
  (106 other events, 539.9 us)
Sparse Core Ops, SparseCore 0:
  15.0 29.6 all-gather.14
  46.8 45.6 all-gather.12
  134.3 42.4 reduce-scatter.16
  178.6 26.9 all-gather.18
  207.5 45.6 all-gather.16
  255.2 44.4 all-gather.22
  301.6 26.5 all-gather.20
  341.8 43.6 reduce-scatter.18
  392.4 44.8 all-gather.24
  439.4 42.4 reduce-scatter.22
  510.6 42.4 reduce-scatter.20
  561.5 26.0 all-gather.14
  589.7 45.6 all-gather.12
  677.3 42.4 reduce-scatter.16
  721.5 26.9 all-gather.18
  750.5 45.6 all-gather.16
  798.2 44.4 all-gather.22
  844.4 26.5 all-gather.20
  884.7 43.6 reduce-scatter.18
  935.2 44.8 all-gather.24
  982.4 42.4 reduce-scatter.22
  1053.4 42.4 reduce-scatter.20
Sparse Core Ops, SparseCore 1:
  1108.6 33.3 reduce-scatter.10
  1145.2 38.2 reduce-scatter.8
  1186.6 41.0 reduce-scatter.12
  1230.9 41.0 reduce-scatter.14
where the time goes:
time: 1290 us; the launch traced here: 1280 us
  waiting for transfers between devices  773 us (60%)
  matrix products  199 us (15%)
  other arithmetic  115 us (9%)
  local copies, waits for them, and re-layouts  104 us (8%)
  blocking collectives  67.2 us (5%)
  between operations  16.3 us (1%)
    all_gather x4, waiting for transfers between devices, seq_gather(): return lax.all_gather(values, 'tensor', axis=0, tiled=True)  191 us
    all_gather x4, waiting for transfers between devices, grad_gather(): return lax.all_gather(values, 'tensor', axis=0, tiled=True)  136 us
    reduce_scatter x4, waiting for transfers between devices, grad_sum(): lax.psum_scatter(values.astype(jnp.bfloat16), 'tensor', scatter_dimension...  127 us
    reduce_scatter x4, waiting for transfers between devices, part_sum(): lax.psum_scatter(values.astype(jnp.bfloat16), 'tensor', scatter_dimension...  83.9 us
    dot_general x16, matrix products, contract(): lax.dot_general(left, right, (((left_dim,), (right_dim,)), ((), ())), pre...  69.9 us
    all_gather x2, waiting for transfers between devices, fetch(): lax.all_gather(fc2_weight, 'dp', axis=0, tiled=True)  56.9 us
    all_gather x2, waiting for transfers between devices, fetch(): lax.all_gather(fc1_weight, 'dp', axis=0, tiled=True)  44.4 us
    reduce_scatter x1, waiting for transfers between devices, body(): lax.psum_scatter(totals[10].astype(jnp.bfloat16), 'dp', scatter_dimension...  42.5 us
  transfers between devices with their start and end apart: 26, of which 23 were waited for; matrix products, arithmetic and copies ran while one was open for 21% of the time, Pallas kernels for 0%

commit v1 on v0

--- a/solution.py
+++ b/solution.py
@@ -6,6 +6,26 @@
 
 HD = 64
 GRID = 16
+
+
+def register_members_all_over_axis(s0):
+    dev_n = lax.psum(1, axis_name="tensor")
+    queue = []
+    for k0 in range(dev_n):
+        queue.append((k0, (k0 + 1) % dev_n))
+    trail = []
+    for k0 in range(dev_n):
+        trail.append((k0, (k0 - 1) % dev_n))
+    after, mixed_arr = ([s0], [s0])
+    for _ in range(dev_n // 2):
+        after.append(lax.ppermute(after[-1], "tensor", queue))
+    for _ in range((dev_n - 1) // 2):
+        mixed_arr.append(lax.ppermute(mixed_arr[-1], axis_name="tensor", perm=trail))
+    return jnp.roll(
+        jnp.concatenate([*after[::-1], *mixed_arr[1:]], 0),
+        (lax.axis_index("tensor") - dev_n // 2) * s0.shape[0],
+        0,
+    )
 
 
 def norm_rows(values, gain_vec, shift_vec):
@@ -104,7 +124,7 @@
         ).astype(jnp.float32)
 
     def grad_gather(values):
-        return lax.all_gather(values, "tensor", axis=0, tiled=True)
+        return register_members_all_over_axis(values)
 
     def grad_sum(values):
         return lax.psum_scatter(

time: 1290 us -> 1200 us (0.930)
  waiting for transfers between devices: 773 us -> 600 us
  other arithmetic: 115 us -> 163 us
  starting transfers between devices: 1.42 us -> 47.4 us
    all_gather x4 -> x0, waiting for transfers between devices: 136 us -> none  [grad_gather(): return lax.all_gather(values, 'tensor', axis=0, tiled=True)]
    ppermute x0 -> x12, waiting for transfers between devices: none -> 95.8 us  [the longest x8 94.6 us: register_members_all_over_axis(): after.append(lax.ppermute(after[-1], 'tensor', queue))]
    all_gather x4, waiting for transfers between devices: 191 us -> 137 us  [seq_gather(): return lax.all_gather(values, 'tensor', axis=0, tiled=True)]
    concatenate x0 -> x4, other arithmetic: none -> 48.1 us  [register_members_all_over_axis(): jnp.roll(jnp.concatenate([*after[::-1], *mixed_arr[1:]], 0), (lax.axis_in...]
    ppermute x0 -> x12, starting transfers between devices: none -> 46 us  [the longest x8 33.3 us: register_members_all_over_axis(): after.append(lax.ppermute(after[-1], 'tensor', queue))]
    all_gather x2, waiting for transfers between devices: 44.4 us -> 0.01 us  [fetch(): lax.all_gather(fc1_weight, 'dp', axis=0, tiled=True)]
    all_gather x2, waiting for transfers between devices: 56.9 us -> 25.3 us  [fetch(): lax.all_gather(fc2_weight, 'dp', axis=0, tiled=True)]
  transfers between devices with their start and end apart: 26 -> 34, of which waited for: 23 -> 27; matrix products, arithmetic and copies ran while one was open for 21% -> 26% of each run, Pallas kernels for 0% -> 0%
where the time goes in v1:
time: 1200 us; the launch traced here: 1190 us
  waiting for transfers between devices  600 us (50%)
  matrix products  192 us (16%)
  other arithmetic  163 us (14%)
  local copies, waits for them, and re-layouts  103 us (9%)
  blocking collectives  67.3 us (6%)
  starting transfers between devices  47.4 us (4%)
  between operations  16.2 us (1%)
    all_gather x4, waiting for transfers between devices, seq_gather(): return lax.all_gather(values, 'tensor', axis=0, tiled=True)  137 us
    reduce_scatter x4, waiting for transfers between devices, grad_sum(): lax.psum_scatter(values.astype(jnp.bfloat16), 'tensor', scatter_dimension...  126 us
    ppermute x8, waiting for transfers between devices, register_members_all_over_axis(): after.append(lax.ppermute(after[-1], 'tensor', queue))  94.6 us
    reduce_scatter x4, waiting for transfers between devices, part_sum(): lax.psum_scatter(values.astype(jnp.bfloat16), 'tensor', scatter_dimension...  83.8 us
    dot_general x16, matrix products, contract(): lax.dot_general(left, right, (((left_dim,), (right_dim,)), ((), ())), pre...  65.4 us
    concatenate x4, other arithmetic, register_members_all_over_axis(): jnp.roll(jnp.concatenate([*after[::-1], *mixed_arr[1:]], 0), (lax.axis_in...  48.1 us
    reduce_scatter x1, waiting for transfers between devices, body(): lax.psum_scatter(totals[10].astype(jnp.bfloat16), 'dp', scatter_dimension...  42.5 us
    reduce_scatter x1, waiting for transfers between devices, body(): lax.psum_scatter(totals[8].astype(jnp.bfloat16), 'dp', scatter_dimension=...  42.5 us
  transfers between devices with their start and end apart: 34, of which 27 were waited for; matrix products, arithmetic and copies ran while one was open for 26% of the time, Pallas kernels for 0%

profile of v1, /device:TPU:0, one launch (start us, length us, event | category | flops | bytes accessed | tf_op | source)
XLA Modules:
  0.0 1194.7 jit_solution(18387007358626220348)
XLA Ops:
  12.3 1005.3 %while.40 = (s32[]{:T(128)}, f32[1024]{0:T(1024)}, f32[1024]{0:T(1024)}, f32[1024,768]{1,0:T(8,128)}, f32[768]{0:T(1024)}, /*index=5*/f32[1024,256]{1,0:T(8,128)...) while((s32[]{:T(128)}, f32[1024]{0:T(1024)}, ...), condition=%wide.wide.region_27.29_spmd.clone, body=%wide.wide.region_0.28_spmd.clone.sunk | while | flops 22808760320 | bytes 767505216 | solution.py:320
  17.9 14.5 %all_gather.60 = bf16[1024,256]{1,0:T(8,128)(2,1)} all-gather(bf16[128,256]{1,0:T(8,128)(2,1)} %get-tuple-element.1164), channel_id=1, replica_groups=mesh['dp'=8,'tensor'=4] {'dp'}, dimensions={0}, use_global_device_ids=true | all-gather | bytes 589824 | tf_op jit(solution)/shard_map/while/body/eval_jaxpr/all_gather | solution.py:112
  32.4 12.2 %all-gather.8.cloned.1.call-done = bf16[1024,768]{1,0:T(8,128)(2,1)} async-done(((bf16[128,768]{1,0:T(8,128)(2,1)}), bf16[1024,768]{1,0:T(8,128)(2,1)}) %all-gather.8.cloned.1.call-update) | async-done | bytes 1572880 | tf_op jit(solution)/shard_map/while/body/eval_jaxpr/all_gather | solution.py:111
  44.7 47.8 %all-gather.6.cloned.1.call-done = bf16[1024,1024]{1,0:T(8,128)(2,1)} async-done(((bf16[256,1024]{1,0:T(8,128)(2,1)}), bf16[1024,1024]{1,0:T(8,128)(2,1)}) %all-gather.6.cloned.1.call-update) | async-done | bytes 2097168 | tf_op jit(solution)/shard_map/while/body/eval_jaxpr/all_gather | solution.py:119
  99.9 5.3 rev.37
  108.6 5.2 rev.36
  134.9 42.0 %reduce-scatter.17.cloned.1.call-done = bf16[256,1024]{1,0:T(8,128)(2,1)} async-done(((bf16[1024,1024]{1,0:T(8,128)(2,1)}), bf16[256,1024]{1,0:T(8,128)(2,1)}) %reduce-scatter.17.cloned.1.call-update) | async-done | bytes 524304 | tf_op jit(solution)/shard_map/while/body/eval_jaxpr/reduce_scatter | solution.py:122
  186.9 12.8 %collective-permute-done = bf16[256,1024]{1,0:T(8,128)(2,1)S(1)} collective-permute-done((bf16[256,1024]{1,0:T(8,128)(2,1)S(1)}, bf16[256,1024]{1,0:T(8,128)(2,1)S(1)}, u32[]{:S(2)}, u32[]{:S(2)}) %collective-permute-start) | collective-permute-done | bytes 524320 | tf_op jit(solution)/shard_map/while/body/eval_jaxpr/ppermute | solution.py:21
  199.6 7.6 collective-permute-start.1
  208.2 14.0 %collective-permute-done.1 = bf16[256,1024]{1,0:T(8,128)(2,1)} collective-permute-done((bf16[256,1024]{1,0:T(8,128)(2,1)S(1)}, bf16[256,1024]{1,0:T(8,128)(2,1)}, u32[]{:S(2)}, u32[]{:S(2)}) %collective-permute-start.1) | collective-permute-done | bytes 524320 | tf_op jit(solution)/shard_map/while/body/eval_jaxpr/ppermute | solution.py:21
  222.2 12.5 %fusion.346 = bf16[1024,1024]{1,0:T(8,128)(2,1)} fusion(s32[]{:T(128)S(6)} %select_n.113, bf16[256,1024]{1,0:T(8,128)(2,1)} %collective-permute-done.1, bf16[256,1024]{1,0:T(8,128)(2,1)S(1)} %collective-permute-done, bf16[256,1024]{1,0:T(8,128)(2,1)S(1)} %get-tuple-element.1033, bf16[256,1024]{1,0:T(8,128)(2,1)S(1)} %collective-permute-done.2), kind=kLoop, calls=%fused_computation.73.clone.clone.1 | loop fusion | flops 16777216 | bytes 4194308 | tf_op jit(solution)/shard_map/while/body/eval_jaxpr/jit(_roll_dynamic)/concatenate | solution.py:24
  234.7 20.5 %all-gather.10.cloned.1.call-done = bf16[1024,1024]{1,0:T(8,128)(2,1)} async-done(((bf16[256,1024]{1,0:T(8,128)(2,1)}), bf16[1024,1024]{1,0:T(8,128)(2,1)}) %all-gather.10.cloned.1.call-update) | async-done | bytes 2097168 | tf_op jit(solution)/shard_map/while/body/eval_jaxpr/all_gather | solution.py:119
  255.2 15.4 %multiply_convert_fusion.9 = (bf16[1024,1024]{1,0:T(8,128)(2,1)}, f32[1024,1024]{1,0:T(8,128)}, f32[1024,1024]{1,0:T(8,128)}) fusion(f32[1024]{0:T(1024)S(1)} %copy-done.72, bf16[1024,1024]{1,0:T(8,128)(2,1)} %all-gather.10.cloned.1.call-done, bf16[1024,1024]{1,0:T(8,128)(2,1)} %all-gather.12.cloned.1.call-done), kind=kOutput, calls=%fused_computation.38.clone.clone.1 | convolution fusion | flops 2216689664 | bytes 14684160 | tf_op jit(solution)/shard_map/while/body/eval_jaxpr/dot_general | solution.py:173
  270.6 12.7 %all-gather.14.cloned.1.call-done = bf16[1024,1024]{1,0:T(8,128)(2,1)} async-done(((bf16[128,1024]{1,0:T(8,128)(2,1)}), bf16[1024,1024]{1,0:T(8,128)(2,1)}) %all-gather.14.cloned.1.call-update) | async-done | bytes 2097168 | tf_op jit(solution)/shard_map/while/body/eval_jaxpr/all_gather | solution.py:114
  283.2 8.4 convert_reduce_fusion.18
  296.8 43.7 %reduce-scatter.19.cloned.1.call-done = bf16[256,1024]{1,0:T(8,128)(2,1)} async-done(((bf16[1024,1024]{1,0:T(8,128)(2,1)}), bf16[256,1024]{1,0:T(8,128)(2,1)}) %reduce-scatter.19.cloned.1.call-update) | async-done | bytes 524304 | tf_op jit(solution)/shard_map/while/body/eval_jaxpr/reduce_scatter | solution.py:130
  352.3 10.9 collective-permute-done.3
  363.3 7.6 collective-permute-start.4
  374.7 9.7 collective-permute-done.4
  384.4 11.6 fusion.349
  397.5 5.5 multiply_reduce_fusion.18
  407.9 6.2 multiply_reduce_fusion.19
  416.6 7.1 multiply_convert_fusion.11
  429.8 4.2 rev.38
  443.4 6.2 rev.39
  456.0 4.5 fusion.351
  467.7 6.1 select_add_fusion.39
  473.9 4.5 select_add_fusion.37
  487.4 22.1 %reduce-scatter.21.cloned.1.call-done = bf16[256,1024]{1,0:T(8,128)(2,1)} async-done(((bf16[1024,1024]{1,0:T(8,128)(2,1)}), bf16[256,1024]{1,0:T(8,128)(2,1)}) %reduce-scatter.21.cloned.1.call-update) | async-done | bytes 524304 | tf_op jit(solution)/shard_map/while/body/eval_jaxpr/reduce_scatter | solution.py:130
  521.0 11.8 all_gather.60
  532.8 11.3 all-gather.8.cloned.1.call-done
  544.1 47.8 %all-gather.6.cloned.1.call-done = bf16[1024,1024]{1,0:T(8,128)(2,1)} async-done(((bf16[256,1024]{1,0:T(8,128)(2,1)}), bf16[1024,1024]{1,0:T(8,128)(2,1)}) %all-gather.6.cloned.1.call-update) | async-done | bytes 2097168 | tf_op jit(solution)/shard_map/while/body/eval_jaxpr/all_gather | solution.py:119
  591.9 3.9 convolution_add_fusion.7
  599.3 5.3 rev.37
  608.0 5.2 rev.36
  634.5 41.8 %reduce-scatter.17.cloned.1.call-done = bf16[256,1024]{1,0:T(8,128)(2,1)} async-done(((bf16[1024,1024]{1,0:T(8,128)(2,1)}), bf16[256,1024]{1,0:T(8,128)(2,1)}) %reduce-scatter.17.cloned.1.call-update) | async-done | bytes 524304 | tf_op jit(solution)/shard_map/while/body/eval_jaxpr/reduce_scatter | solution.py:122
  686.3 12.8 %collective-permute-done = bf16[256,1024]{1,0:T(8,128)(2,1)S(1)} collective-permute-done((bf16[256,1024]{1,0:T(8,128)(2,1)S(1)}, bf16[256,1024]{1,0:T(8,128)(2,1)S(1)}, u32[]{:S(2)}, u32[]{:S(2)}) %collective-permute-start) | collective-permute-done | bytes 524320 | tf_op jit(solution)/shard_map/while/body/eval_jaxpr/ppermute | solution.py:21
  699.1 7.6 collective-permute-start.1
  707.6 13.8 %collective-permute-done.1 = bf16[256,1024]{1,0:T(8,128)(2,1)} collective-permute-done((bf16[256,1024]{1,0:T(8,128)(2,1)S(1)}, bf16[256,1024]{1,0:T(8,128)(2,1)}, u32[]{:S(2)}, u32[]{:S(2)}) %collective-permute-start.1) | collective-permute-done | bytes 524320 | tf_op jit(solution)/shard_map/while/body/eval_jaxpr/ppermute | solution.py:21
  721.4 12.5 %fusion.346 = bf16[1024,1024]{1,0:T(8,128)(2,1)} fusion(s32[]{:T(128)S(6)} %select_n.113, bf16[256,1024]{1,0:T(8,128)(2,1)} %collective-permute-done.1, bf16[256,1024]{1,0:T(8,128)(2,1)S(1)} %collective-permute-done, bf16[256,1024]{1,0:T(8,128)(2,1)S(1)} %get-tuple-element.1033, bf16[256,1024]{1,0:T(8,128)(2,1)S(1)} %collective-permute-done.2), kind=kLoop, calls=%fused_computation.73.clone.clone.1 | loop fusion | flops 16777216 | bytes 4194308 | tf_op jit(solution)/shard_map/while/body/eval_jaxpr/jit(_roll_dynamic)/concatenate | solution.py:24
  733.9 20.7 %all-gather.10.cloned.1.call-done = bf16[1024,1024]{1,0:T(8,128)(2,1)} async-done(((bf16[256,1024]{1,0:T(8,128)(2,1)}), bf16[1024,1024]{1,0:T(8,128)(2,1)}) %all-gather.10.cloned.1.call-update) | async-done | bytes 2097168 | tf_op jit(solution)/shard_map/while/body/eval_jaxpr/all_gather | solution.py:119
  754.6 15.4 %multiply_convert_fusion.9 = (bf16[1024,1024]{1,0:T(8,128)(2,1)}, f32[1024,1024]{1,0:T(8,128)}, f32[1024,1024]{1,0:T(8,128)}) fusion(f32[1024]{0:T(1024)S(1)} %copy-done.72, bf16[1024,1024]{1,0:T(8,128)(2,1)} %all-gather.10.cloned.1.call-done, bf16[1024,1024]{1,0:T(8,128)(2,1)} %all-gather.12.cloned.1.call-done), kind=kOutput, calls=%fused_computation.38.clone.clone.1 | convolution fusion | flops 2216689664 | bytes 14684160 | tf_op jit(solution)/shard_map/while/body/eval_jaxpr/dot_general | solution.py:173
  770.0 12.6 %all-gather.14.cloned.1.call-done = bf16[1024,1024]{1,0:T(8,128)(2,1)} async-done(((bf16[128,1024]{1,0:T(8,128)(2,1)}), bf16[1024,1024]{1,0:T(8,128)(2,1)}) %all-gather.14.cloned.1.call-update) | async-done | bytes 2097168 | tf_op jit(solution)/shard_map/while/body/eval_jaxpr/all_gather | solution.py:114
  782.6 8.4 convert_reduce_fusion.18
  796.2 43.7 %reduce-scatter.19.cloned.1.call-done = bf16[256,1024]{1,0:T(8,128)(2,1)} async-done(((bf16[1024,1024]{1,0:T(8,128)(2,1)}), bf16[256,1024]{1,0:T(8,128)(2,1)}) %reduce-scatter.19.cloned.1.call-update) | async-done | bytes 524304 | tf_op jit(solution)/shard_map/while/body/eval_jaxpr/reduce_scatter | solution.py:130
  851.8 10.9 collective-permute-done.3
  862.7 7.6 collective-permute-start.4
  874.1 9.7 collective-permute-done.4
  883.8 11.6 fusion.349
  896.9 5.5 multiply_reduce_fusion.18
  907.3 6.2 multiply_reduce_fusion.19
  916.0 7.1 multiply_convert_fusion.11
  929.2 4.2 rev.38
  942.8 6.2 rev.39
  955.4 4.5 fusion.351
  967.1 7.3 select_add_fusion.39
  974.5 6.9 select_add_fusion.37
  986.8 5.8 select_add_fusion.33
  992.5 16.4 %reduce-scatter.21.cloned.1.call-done = bf16[256,1024]{1,0:T(8,128)(2,1)} async-done(((bf16[1024,1024]{1,0:T(8,128)(2,1)}), bf16[256,1024]{1,0:T(8,128)(2,1)}) %reduce-scatter.21.cloned.1.call-update) | async-done | bytes 524304 | tf_op jit(solution)/shard_map/while/body/eval_jaxpr/reduce_scatter | solution.py:130
  1027.1 4.0 convert_element_type.260
  1031.8 41.0 %all-reduce = (f32[1024]{0:T(1024)}, f32[1024]{0:T(1024)}, f32[3072]{0:T(1024)S(1)}, f32[1024]{0:T(1024)}, f32[1024]{0:T(1024)}, /*index=5*/f32[1024]{0:T(1024)}, f32[4096]{0:T(1024)S(1)}, f32[1024]{0:T(1024)}) all-reduce(f32[1024]{0:T(1024)S(1)} %copy-done.64, ...), channel_id=1, replica_groups=mesh['dp'=8,'tensor'=4] {'dp','tensor'}, use_global_device_ids=true, to_apply=%region_28.30 | all-reduce | flops 13312 | bytes 106496 | tf_op jit(solution)/shard_map/psum | solution.py:345
  1075.5 21.1 %reduce-scatter.9.cloned.1.call-done = bf16[128,768]{1,0:T(8,128)(2,1)} async-done(((bf16[1024,768]{1,0:T(8,128)(2,1)}), bf16[128,768]{1,0:T(8,128)(2,1)}) %reduce-scatter.9.cloned.1.call-update) | async-done | bytes 196624 | tf_op jit(solution)/shard_map/reduce_scatter | solution.py:323
  1098.3 42.5 %reduce-scatter.13.cloned.1.call-done = bf16[128,1024]{1,0:T(8,128)(2,1)} async-done(((bf16[1024,1024]{1,0:T(8,128)(2,1)}), bf16[128,1024]{1,0:T(8,128)(2,1)}) %reduce-scatter.13.cloned.1.call-update) | async-done | bytes 262160 | tf_op jit(solution)/shard_map/reduce_scatter | solution.py:329
  1142.6 42.5 %reduce-scatter.15.cloned.1.call-done = bf16[128,1024]{1,0:T(8,128)(2,1)} async-done(((bf16[1024,1024]{1,0:T(8,128)(2,1)}), bf16[128,1024]{1,0:T(8,128)(2,1)}) %reduce-scatter.15.cloned.1.call-update) | async-done | bytes 262160 | tf_op jit(solution)/shard_map/reduce_scatter | solution.py:332
  (565 shorter events, 256.2 us)
Async XLA Ops:
  12.3 335.0 %copy-start.19 = (f32[1024,1,64]{0,2,1:T(8,128)}, f32[1024,1,64]{0,2,1:T(8,128)S(1)}, u32[]{:S(2)}) copy-start(f32[1024,1,64]{0,2,1:T(8,128)S(1)} %get-tuple-element.1161) | copy-start | bytes 786436 | tf_op jit(solution)/shard_map/while
  12.3 32.3 %all-gather.8.cloned.1.call-start = ((), (), s32[]{:S(2)}) async-start(), calls=%async_computation.13 | async-start | bytes 1769472 | tf_op jit(solution)/shard_map/while/body/eval_jaxpr/all_gather | solution.py:111
  13.1 79.4 %all-gather.6.cloned.1.call-start = ((), (), s32[]{:S(2)}) async-start(), calls=%async_computation.12 | async-start | bytes 2621440 | tf_op jit(solution)/shard_map/while/body/eval_jaxpr/all_gather | solution.py:119
  14.3 82.1 %copy-start.35 = (f32[256]{0:T(256)}, f32[256]{0:T(256)S(1)}, u32[]{:S(2)}) copy-start(f32[256]{0:T(256)S(1)} %broadcast_multiply_fusion.16) | copy-start | bytes 3076 | tf_op jit(solution)/shard_map/while
  15.7 80.8 %copy-start.39 = (f32[256]{0:T(256)}, f32[256]{0:T(256)S(1)}, u32[]{:S(2)}) copy-start(f32[256]{0:T(256)S(1)} %fusion.335) | copy-start | bytes 3076 | tf_op jit(solution)/shard_map/while
  15.7 80.8 %copy-start.37 = (f32[256]{0:T(256)}, f32[256]{0:T(256)S(1)}, u32[]{:S(2)}) copy-start(f32[256]{0:T(256)S(1)} %fusion.336) | copy-start | bytes 3076 | tf_op jit(solution)/shard_map/while
  17.9 159.0 %reduce-scatter.17.cloned.1.call-start = ((), (), s32[]{:S(2)}) async-start(), calls=%async_computation.14 | async-start | bytes 2621440 | tf_op jit(solution)/shard_map/while/body/eval_jaxpr/reduce_scatter | solution.py:122
  131.2 45.6 %copy-start.2 = (bf16[2,256,1024]{2,1,0:T(8,128)(2,1)S(1)}, bf16[2,256,1024]{2,1,0:T(8,128)(2,1)}, u32[]{:S(2)}) copy-start(bf16[2,256,1024]{2,1,0:T(8,128)(2,1)} %get-tuple-element.1156) | copy-start | bytes 3145732 | tf_op jit(solution)/shard_map/while
  131.3 45.6 %copy-start.32 = (f32[1024]{0:T(1024)S(1)}, f32[1024]{0:T(1024)}, u32[]{:S(2)}) copy-start(f32[1024]{0:T(1024)} %get-tuple-element.1165) | copy-start | bytes 12292 | tf_op jit(solution)/shard_map/while
  131.3 48.3 %copy-start.34 = (f32[1024]{0:T(1024)S(1)}, f32[1024]{0:T(1024)}, u32[]{:S(2)}) copy-start(f32[1024]{0:T(1024)} %get-tuple-element.1166) | copy-start | bytes 12292 | tf_op jit(solution)/shard_map/while
  131.3 48.3 %copy-start.65 = (f32[1024]{0:T(1024)S(1)}, f32[1024]{0:T(1024)}, u32[]{:S(2)}) copy-start(f32[1024]{0:T(1024)} %get-tuple-element.1167) | copy-start | bytes 12292 | tf_op jit(solution)/shard_map/while
  134.3 100.4 %all-gather.12.cloned.1.call-start = ((), (), s32[]{:S(2)}) async-start(), calls=%async_computation.16 | async-start | bytes 2359296 | tf_op jit(solution)/shard_map/while/body/eval_jaxpr/all_gather | solution.py:113
  134.9 120.3 %all-gather.10.cloned.1.call-start = ((), (), s32[]{:S(2)}) async-start(), calls=%async_computation.15 | async-start | bytes 2621440 | tf_op jit(solution)/shard_map/while/body/eval_jaxpr/all_gather | solution.py:119
  178.2 77.0 %copy-start.72 = (f32[1024]{0:T(1024)S(1)}, f32[1024]{0:T(1024)}, u32[]{:S(2)}) copy-start(f32[1024]{0:T(1024)} %get-tuple-element.1169) | copy-start | bytes 12292 | tf_op jit(solution)/shard_map/while
  181.8 101.4 %all-gather.14.cloned.1.call-start = ((), (), s32[]{:S(2)}) async-start(), calls=%async_computation.17 | async-start | bytes 2359296 | tf_op jit(solution)/shard_map/while/body/eval_jaxpr/all_gather | solution.py:114
  183.0 16.6 %collective-permute-start = (bf16[256,1024]{1,0:T(8,128)(2,1)S(1)}, bf16[256,1024]{1,0:T(8,128)(2,1)S(1)}, u32[]{:S(2)}, u32[]{:S(2)}) collective-permute-start(bf16[256,1024]{1,0:T(8,128)(2,1)S(1)} %get-tuple-element.1033), channel_id=1, source_target_pairs={{0,1},{1,2},{2,3},{3,0},{4,5},{5,6},{6,7},{7,4},{8,9},{9,10},{10,1... | collective-permute-start | bytes 1572872 | tf_op jit(solution)/shard_map/while/body/eval_jaxpr/ppermute | solution.py:21
  183.7 24.5 %collective-permute-start.2 = (bf16[256,1024]{1,0:T(8,128)(2,1)S(1)}, bf16[256,1024]{1,0:T(8,128)(2,1)S(1)}, u32[]{:S(2)}, u32[]{:S(2)}) collective-permute-start(bf16[256,1024]{1,0:T(8,128)(2,1)S(1)} %get-tuple-element.1033), channel_id=1, source_target_pairs={{0,3},{1,0},{2,1},{3,2},{4,7},{5,4},{6,5},{7,6},{8,11},{9,8},{10,9... | collective-permute-start | bytes 1572872 | tf_op jit(solution)/shard_map/while/body/eval_jaxpr/ppermute | solution.py:23
  199.6 22.6 %collective-permute-start.1 = (bf16[256,1024]{1,0:T(8,128)(2,1)S(1)}, bf16[256,1024]{1,0:T(8,128)(2,1)}, u32[]{:S(2)}, u32[]{:S(2)}) collective-permute-start(bf16[256,1024]{1,0:T(8,128)(2,1)S(1)} %collective-permute-done), channel_id=1, source_target_pairs={{0,1},{1,2},{2,3},{3,0},{4,5},{5,6},{6,7},{7,4},{8,9},{9,10},{10,1... | collective-permute-start | bytes 1572872 | tf_op jit(solution)/shard_map/while/body/eval_jaxpr/ppermute | solution.py:21
  207.3 133.2 %reduce-scatter.19.cloned.1.call-start = ((), (), s32[]{:S(2)}) async-start(), calls=%async_computation.18 | async-start | bytes 2621440 | tf_op jit(solution)/shard_map/while/body/eval_jaxpr/reduce_scatter | solution.py:130
  293.0 47.5 %copy-start.4 = (bf16[256,1024]{1,0:T(8,128)(2,1)S(1)}, bf16[256,1024]{1,0:T(8,128)(2,1)}, u32[]{:S(2)}) copy-start(bf16[256,1024]{1,0:T(8,128)(2,1)} %reduce-scatter.17.cloned.1.call-done) | copy-start | bytes 1572868 | tf_op jit(solution)/shard_map/while
  296.8 181.8 %reduce-scatter.23.cloned.1.call-start = ((), (), s32[]{:S(2)}) async-start(), calls=%async_computation.20 | async-start | bytes 2621440 | tf_op jit(solution)/shard_map/while/body/eval_jaxpr/reduce_scatter | solution.py:122
  340.5 30.4 %copy-start.69 = (bf16[1024,1024]{1,0:T(8,128)(2,1)S(1)}, bf16[1024,1024]{1,0:T(8,128)(2,1)}, u32[]{:S(2)}) copy-start(bf16[1024,1024]{1,0:T(8,128)(2,1)} %all-gather.14.cloned.1.call-done) | copy-start | bytes 6291460 | tf_op jit(solution)/shard_map/while
  340.5 30.4 %copy-start.73 = (bf16[1024,1024]{1,0:T(8,128)(2,1)S(1)}, bf16[1024,1024]{1,0:T(8,128)(2,1)}, u32[]{:S(2)}) copy-start(bf16[1024,1024]{1,0:T(8,128)(2,1)} %get-tuple-element.1058) | copy-start | bytes 6291460 | tf_op jit(solution)/shard_map/while
  346.6 16.7 %collective-permute-start.3 = (bf16[256,1024]{1,0:T(8,128)(2,1)S(1)}, bf16[256,1024]{1,0:T(8,128)(2,1)S(1)}, u32[]{:S(2)}, u32[]{:S(2)}) collective-permute-start(bf16[256,1024]{1,0:T(8,128)(2,1)S(1)} %convert_element_type.591), channel_id=1, source_target_pairs={{0,1},{1,2},{2,3},{3,0},{4,5},{5,6},{6,7},{7,4},{8,9},{9,10},{10,1... | collective-permute-start | bytes 1572872 | tf_op jit(solution)/shard_map/while/body/eval_jaxpr/ppermute | solution.py:21
  349.1 25.6 %collective-permute-start.5 = (bf16[256,1024]{1,0:T(8,128)(2,1)S(1)}, bf16[256,1024]{1,0:T(8,128)(2,1)S(1)}, u32[]{:S(2)}, u32[]{:S(2)}) collective-permute-start(bf16[256,1024]{1,0:T(8,128)(2,1)S(1)} %convert_element_type.591), channel_id=1, source_target_pairs={{0,3},{1,0},{2,1},{3,2},{4,7},{5,4},{6,5},{7,6},{8,11},{9,8},{10,9... | collective-permute-start | bytes 1572872 | tf_op jit(solution)/shard_map/while/body/eval_jaxpr/ppermute | solution.py:23
  363.3 21.1 %collective-permute-start.4 = (bf16[256,1024]{1,0:T(8,128)(2,1)S(1)}, bf16[256,1024]{1,0:T(8,128)(2,1)}, u32[]{:S(2)}, u32[]{:S(2)}) collective-permute-start(bf16[256,1024]{1,0:T(8,128)(2,1)S(1)} %collective-permute-done.3), channel_id=1, source_target_pairs={{0,1},{1,2},{2,3},{3,0},{4,5},{5,6},{6,7},{7,4},{8,9},{9,10},{10,1... | collective-permute-start | bytes 1572872 | tf_op jit(solution)/shard_map/while/body/eval_jaxpr/ppermute | solution.py:21
  374.7 134.9 %reduce-scatter.21.cloned.1.call-start = ((), (), s32[]{:S(2)}) async-start(), calls=%async_computation.19 | async-start | bytes 2621440 | tf_op jit(solution)/shard_map/while/body/eval_jaxpr/reduce_scatter | solution.py:130
  483.8 25.8 %copy-start.33 = (f32[1024]{0:T(1024)S(1)}, f32[1024]{0:T(1024)}, u32[]{:S(2)}) copy-start(f32[1024]{0:T(1024)} %get-tuple-element.1157) | copy-start | bytes 12292 | tf_op jit(solution)/shard_map/while
  483.8 27.1 %copy-start.40 = (f32[256]{0:T(256)S(1)}, f32[256]{0:T(256)}, u32[]{:S(2)}) copy-start(f32[256]{0:T(256)} %copy-done.39) | copy-start | bytes 3076 | tf_op jit(solution)/shard_map/while
  483.8 27.1 %copy-start.38 = (f32[256]{0:T(256)S(1)}, f32[256]{0:T(256)}, u32[]{:S(2)}) copy-start(f32[256]{0:T(256)} %copy-done.37) | copy-start | bytes 3076 | tf_op jit(solution)/shard_map/while
  483.8 28.8 %copy-start.62 = (f32[1024]{0:T(1024)S(1)}, f32[1024]{0:T(1024)}, u32[]{:S(2)}) copy-start(f32[1024]{0:T(1024)} %get-tuple-element.1102) | copy-start | bytes 12292 | tf_op jit(solution)/shard_map/while
  483.8 28.8 %copy-start.59 = (f32[1024]{0:T(1024)S(1)}, f32[1024]{0:T(1024)}, u32[]{:S(2)}) copy-start(f32[1024]{0:T(1024)} %get-tuple-element.1103) | copy-start | bytes 12292 | tf_op jit(solution)/shard_map/while
  483.9 28.8 %copy-start.10 = (f32[256,1024]{1,0:T(8,128)S(1)}, f32[256,1024]{1,0:T(8,128)}, u32[]{:S(2)}) copy-start(f32[256,1024]{1,0:T(8,128)} %copy-done.9) | copy-start | bytes 3145732 | tf_op jit(solution)/shard_map/while
  515.5 331.1 %copy-start.19 = (f32[1024,1,64]{0,2,1:T(8,128)}, f32[1024,1,64]{0,2,1:T(8,128)S(1)}, u32[]{:S(2)}) copy-start(f32[1024,1,64]{0,2,1:T(8,128)S(1)} %get-tuple-element.1161) | copy-start | bytes 786436 | tf_op jit(solution)/shard_map/while
  515.6 28.5 %all-gather.8.cloned.1.call-start = ((), (), s32[]{:S(2)}) async-start(), calls=%async_computation.13 | async-start | bytes 1769472 | tf_op jit(solution)/shard_map/while/body/eval_jaxpr/all_gather | solution.py:111
  516.1 75.8 %all-gather.6.cloned.1.call-start = ((), (), s32[]{:S(2)}) async-start(), calls=%async_computation.12 | async-start | bytes 2621440 | tf_op jit(solution)/shard_map/while/body/eval_jaxpr/all_gather | solution.py:119
  517.4 78.5 %copy-start.35 = (f32[256]{0:T(256)}, f32[256]{0:T(256)S(1)}, u32[]{:S(2)}) copy-start(f32[256]{0:T(256)S(1)} %broadcast_multiply_fusion.16) | copy-start | bytes 3076 | tf_op jit(solution)/shard_map/while
  518.7 77.1 %copy-start.39 = (f32[256]{0:T(256)}, f32[256]{0:T(256)S(1)}, u32[]{:S(2)}) copy-start(f32[256]{0:T(256)S(1)} %fusion.335) | copy-start | bytes 3076 | tf_op jit(solution)/shard_map/while
  518.8 77.1 %copy-start.37 = (f32[256]{0:T(256)}, f32[256]{0:T(256)S(1)}, u32[]{:S(2)}) copy-start(f32[256]{0:T(256)S(1)} %fusion.336) | copy-start | bytes 3076 | tf_op jit(solution)/shard_map/while
  520.9 155.4 %reduce-scatter.17.cloned.1.call-start = ((), (), s32[]{:S(2)}) async-start(), calls=%async_computation.14 | async-start | bytes 2621440 | tf_op jit(solution)/shard_map/while/body/eval_jaxpr/reduce_scatter | solution.py:122
  630.7 45.7 %copy-start.2 = (bf16[2,256,1024]{2,1,0:T(8,128)(2,1)S(1)}, bf16[2,256,1024]{2,1,0:T(8,128)(2,1)}, u32[]{:S(2)}) copy-start(bf16[2,256,1024]{2,1,0:T(8,128)(2,1)} %get-tuple-element.1156) | copy-start | bytes 3145732 | tf_op jit(solution)/shard_map/while
  630.7 45.6 %copy-start.32 = (f32[1024]{0:T(1024)S(1)}, f32[1024]{0:T(1024)}, u32[]{:S(2)}) copy-start(f32[1024]{0:T(1024)} %get-tuple-element.1165) | copy-start | bytes 12292 | tf_op jit(solution)/shard_map/while
  630.7 48.3 %copy-start.34 = (f32[1024]{0:T(1024)S(1)}, f32[1024]{0:T(1024)}, u32[]{:S(2)}) copy-start(f32[1024]{0:T(1024)} %get-tuple-element.1166) | copy-start | bytes 12292 | tf_op jit(solution)/shard_map/while
  630.7 48.3 %copy-start.65 = (f32[1024]{0:T(1024)S(1)}, f32[1024]{0:T(1024)}, u32[]{:S(2)}) copy-start(f32[1024]{0:T(1024)} %get-tuple-element.1167) | copy-start | bytes 12292 | tf_op jit(solution)/shard_map/while
  633.7 100.1 %all-gather.12.cloned.1.call-start = ((), (), s32[]{:S(2)}) async-start(), calls=%async_computation.16 | async-start | bytes 2359296 | tf_op jit(solution)/shard_map/while/body/eval_jaxpr/all_gather | solution.py:113
  634.5 120.1 %all-gather.10.cloned.1.call-start = ((), (), s32[]{:S(2)}) async-start(), calls=%async_computation.15 | async-start | bytes 2621440 | tf_op jit(solution)/shard_map/while/body/eval_jaxpr/all_gather | solution.py:119
  677.6 77.0 %copy-start.72 = (f32[1024]{0:T(1024)S(1)}, f32[1024]{0:T(1024)}, u32[]{:S(2)}) copy-start(f32[1024]{0:T(1024)} %get-tuple-element.1169) | copy-start | bytes 12292 | tf_op jit(solution)/shard_map/while
  681.2 101.4 %all-gather.14.cloned.1.call-start = ((), (), s32[]{:S(2)}) async-start(), calls=%async_computation.17 | async-start | bytes 2359296 | tf_op jit(solution)/shard_map/while/body/eval_jaxpr/all_gather | solution.py:114
  682.4 16.6 %collective-permute-start = (bf16[256,1024]{1,0:T(8,128)(2,1)S(1)}, bf16[256,1024]{1,0:T(8,128)(2,1)S(1)}, u32[]{:S(2)}, u32[]{:S(2)}) collective-permute-start(bf16[256,1024]{1,0:T(8,128)(2,1)S(1)} %get-tuple-element.1033), channel_id=1, source_target_pairs={{0,1},{1,2},{2,3},{3,0},{4,5},{5,6},{6,7},{7,4},{8,9},{9,10},{10,1... | collective-permute-start | bytes 1572872 | tf_op jit(solution)/shard_map/while/body/eval_jaxpr/ppermute | solution.py:21
  683.1 24.5 %collective-permute-start.2 = (bf16[256,1024]{1,0:T(8,128)(2,1)S(1)}, bf16[256,1024]{1,0:T(8,128)(2,1)S(1)}, u32[]{:S(2)}, u32[]{:S(2)}) collective-permute-start(bf16[256,1024]{1,0:T(8,128)(2,1)S(1)} %get-tuple-element.1033), channel_id=1, source_target_pairs={{0,3},{1,0},{2,1},{3,2},{4,7},{5,4},{6,5},{7,6},{8,11},{9,8},{10,9... | collective-permute-start | bytes 1572872 | tf_op jit(solution)/shard_map/while/body/eval_jaxpr/ppermute | solution.py:23
  699.1 22.3 %collective-permute-start.1 = (bf16[256,1024]{1,0:T(8,128)(2,1)S(1)}, bf16[256,1024]{1,0:T(8,128)(2,1)}, u32[]{:S(2)}, u32[]{:S(2)}) collective-permute-start(bf16[256,1024]{1,0:T(8,128)(2,1)S(1)} %collective-permute-done), channel_id=1, source_target_pairs={{0,1},{1,2},{2,3},{3,0},{4,5},{5,6},{6,7},{7,4},{8,9},{9,10},{10,1... | collective-permute-start | bytes 1572872 | tf_op jit(solution)/shard_map/while/body/eval_jaxpr/ppermute | solution.py:21
  706.7 133.3 %reduce-scatter.19.cloned.1.call-start = ((), (), s32[]{:S(2)}) async-start(), calls=%async_computation.18 | async-start | bytes 2621440 | tf_op jit(solution)/shard_map/while/body/eval_jaxpr/reduce_scatter | solution.py:130
  792.4 47.6 %copy-start.4 = (bf16[256,1024]{1,0:T(8,128)(2,1)S(1)}, bf16[256,1024]{1,0:T(8,128)(2,1)}, u32[]{:S(2)}) copy-start(bf16[256,1024]{1,0:T(8,128)(2,1)} %reduce-scatter.17.cloned.1.call-done) | copy-start | bytes 1572868 | tf_op jit(solution)/shard_map/while
  796.2 185.3 %reduce-scatter.23.cloned.1.call-start = ((), (), s32[]{:S(2)}) async-start(), calls=%async_computation.20 | async-start | bytes 2621440 | tf_op jit(solution)/shard_map/while/body/eval_jaxpr/reduce_scatter | solution.py:122
  840.0 30.3 %copy-start.69 = (bf16[1024,1024]{1,0:T(8,128)(2,1)S(1)}, bf16[1024,1024]{1,0:T(8,128)(2,1)}, u32[]{:S(2)}) copy-start(bf16[1024,1024]{1,0:T(8,128)(2,1)} %all-gather.14.cloned.1.call-done) | copy-start | bytes 6291460 | tf_op jit(solution)/shard_map/while
  840.0 30.3 %copy-start.73 = (bf16[1024,1024]{1,0:T(8,128)(2,1)S(1)}, bf16[1024,1024]{1,0:T(8,128)(2,1)}, u32[]{:S(2)}) copy-start(bf16[1024,1024]{1,0:T(8,128)(2,1)} %get-tuple-element.1058) | copy-start | bytes 6291460 | tf_op jit(solution)/shard_map/while
  846.0 16.7 %collective-permute-start.3 = (bf16[256,1024]{1,0:T(8,128)(2,1)S(1)}, bf16[256,1024]{1,0:T(8,128)(2,1)S(1)}, u32[]{:S(2)}, u32[]{:S(2)}) collective-permute-start(bf16[256,1024]{1,0:T(8,128)(2,1)S(1)} %convert_element_type.591), channel_id=1, source_target_pairs={{0,1},{1,2},{2,3},{3,0},{4,5},{5,6},{6,7},{7,4},{8,9},{9,10},{10,1... | collective-permute-start | bytes 1572872 | tf_op jit(solution)/shard_map/while/body/eval_jaxpr/ppermute | solution.py:21
  848.5 25.6 %collective-permute-start.5 = (bf16[256,1024]{1,0:T(8,128)(2,1)S(1)}, bf16[256,1024]{1,0:T(8,128)(2,1)S(1)}, u32[]{:S(2)}, u32[]{:S(2)}) collective-permute-start(bf16[256,1024]{1,0:T(8,128)(2,1)S(1)} %convert_element_type.591), channel_id=1, source_target_pairs={{0,3},{1,0},{2,1},{3,2},{4,7},{5,4},{6,5},{7,6},{8,11},{9,8},{10,9... | collective-permute-start | bytes 1572872 | tf_op jit(solution)/shard_map/while/body/eval_jaxpr/ppermute | solution.py:23
  862.7 21.1 %collective-permute-start.4 = (bf16[256,1024]{1,0:T(8,128)(2,1)S(1)}, bf16[256,1024]{1,0:T(8,128)(2,1)}, u32[]{:S(2)}, u32[]{:S(2)}) collective-permute-start(bf16[256,1024]{1,0:T(8,128)(2,1)S(1)} %collective-permute-done.3), channel_id=1, source_target_pairs={{0,1},{1,2},{2,3},{3,0},{4,5},{5,6},{6,7},{7,4},{8,9},{9,10},{10,1... | collective-permute-start | bytes 1572872 | tf_op jit(solution)/shard_map/while/body/eval_jaxpr/ppermute | solution.py:21
  874.1 134.9 %reduce-scatter.21.cloned.1.call-start = ((), (), s32[]{:S(2)}) async-start(), calls=%async_computation.19 | async-start | bytes 2621440 | tf_op jit(solution)/shard_map/while/body/eval_jaxpr/reduce_scatter | solution.py:130
  1017.6 56.4 %reduce-scatter.11.cloned.1.call-start = ((), (), s32[]{:S(2)}) async-start(), calls=%async_computation.9 | async-start | bytes 589824 | tf_op jit(solution)/shard_map/reduce_scatter | solution.py:326
  1019.8 76.8 %reduce-scatter.9.cloned.1.call-start = ((), (), s32[]{:S(2)}) async-start(), calls=%async_computation.8 | async-start | bytes 1769472 | tf_op jit(solution)/shard_map/reduce_scatter | solution.py:323
  1023.0 117.8 %reduce-scatter.13.cloned.1.call-start = ((), (), s32[]{:S(2)}) async-start(), calls=%async_computation.10 | async-start | bytes 2359296 | tf_op jit(solution)/shard_map/reduce_scatter | solution.py:329
  1027.0 158.1 %reduce-scatter.15.cloned.1.call-start = ((), (), s32[]{:S(2)}) async-start(), calls=%async_computation.11 | async-start | bytes 2359296 | tf_op jit(solution)/shard_map/reduce_scatter | solution.py:332
  (126 other events, 786.3 us)
Sparse Core Ops, SparseCore 0:
  15.0 29.6 all-gather.7
  46.8 45.6 all-gather.5
  134.4 42.4 reduce-scatter.16
  178.6 26.9 all-gather.11
  207.6 47.4 all-gather.9
  256.9 26.2 all-gather.13
  296.9 43.6 reduce-scatter.18
  374.8 44.2 reduce-scatter.22
  467.7 41.7 reduce-scatter.20
  517.9 26.0 all-gather.7
  546.2 45.6 all-gather.5
  633.8 42.4 reduce-scatter.16
  678.2 26.9 all-gather.11
  707.2 47.3 all-gather.9
  756.3 26.2 all-gather.13
  796.3 43.6 reduce-scatter.18
  874.2 44.2 reduce-scatter.22
  967.1 41.7 reduce-scatter.20
Sparse Core Ops, SparseCore 1:
  1021.7 33.4 reduce-scatter.10
  1058.3 38.2 reduce-scatter.8
  1099.8 41.0 reduce-scatter.12
  1144.1 41.0 reduce-scatter.14
